TPU v7x, 256 devices: a whole 4x4x8 slice. The times are simulated.
256 devices in a mesh: tm: 32 (over z_lo, x, core), lat: 8 (over z_hi, y).
Axes of the slice: x: 4, y: 4, z: 8 (z_hi: 2, z_lo: 4; z = z_hi * 4 + z_lo), core: 2. Of those that a mesh axis runs over, the one named last changes fastest.
Arguments:
- first_guess: float32 [32, 69, 64, 512], P('tm', None, 'lat'), may hold values from -6 to 6
- background: float32 [69, 64, 512], P(None, 'lat'), may hold values from -6 to 6
- observed: float32 [32, 69, 64, 512], P('tm', None, 'lat'), may hold values from -6 to 6
- cell_mask: int32 [32, 64, 512], P('tm', 'lat'), may hold values 0 or 1
- chan_mask: int32 [32, 69], P('tm'), may hold values 0 or 1
- w_in: bfloat16 [9, 128, 69], replicated, may hold values from -0.25 to 0.25
- b_in: float32 [128], replicated, may hold values from -3 to 3
- w_out: bfloat16 [9, 69, 128], replicated, may hold values from -0.1875 to 0.1875
Outputs:
- analysis: float32 [32, 69, 64, 512], P('tm', None, 'lat')
All inputs are finite; a program needn't handle non-finite values. No bound on the sum of `cell_mask` or of `chan_mask` on one device may be relied on, other than what follows from the above.
Results may differ from a plain program's by a relative error of at most 0.0037.
Values may be sent and summed in bfloat16 or wider, within the bound.
No kernel may reach another device: no remote copies, remote signals or barrier semaphores. Data moves between devices by JAX's collectives and lax.ppermute only.
A program may use at most 64 MiB of HBM per device.

v0:
```python
import jax
import jax.numpy as jnp
from jax import lax
from jax.experimental import pallas as pl
from jax.experimental.pallas import tpu as pltpu
from jax.sharding import PartitionSpec as P

ITERS = 2
STEP = 0.25
CF = 72
CB = 80
VMEM = pl.BlockSpec(memory_space=pltpu.VMEM)
SMEM = pl.BlockSpec(memory_space=pltpu.SMEM)
F32, BF16 = jnp.float32, jnp.bfloat16


def dot(a, b):
    return jnp.dot(a, b, preferred_element_type=F32)


def shifted_sum(y):
    lon = y.shape[1]
    left = pltpu.roll(y[:CF], 1, 1)
    right = pltpu.roll(y[2 * CF :], lon - 1, 1)
    return y[CF : 2 * CF] + left + right


def place_row(dst, j, row):
    x = row.astype(F32)
    lon = x.shape[1]
    pad = jnp.zeros((CB - x.shape[0], lon), F32)
    for i, v in enumerate((pltpu.roll(x, 1, 1), x, pltpu.roll(x, lon - 1, 1))):
        dst[pl.ds((3 * j + i) * CB, CB), :] = jnp.concatenate([v, pad], axis=0).astype(BF16)


def window(ref, j, unit):
    return ref[pl.ds(j * unit, 3 * unit), :]


def halos(flags, far, near, i):
    odd = flags[4] > 0.5
    a, b = far[i].astype(F32), near[i].astype(F32)
    return jnp.where(odd, b, a), jnp.where(odd, a, b)


def send_edges(flags, rows, far_out, near_out):
    odd = flags[4] > 0.5
    for i in range(2):
        low, high = rows[i], rows[2 + i]
        far_out[i] = jnp.where(odd, high, low).astype(BF16)
        near_out[i] = jnp.where(odd, low, high).astype(BF16)


def inner_forward(own, state, wup, bias, wdn, fore_out, acts_out, slope_out, xs, acts):
    n, hid = own.shape[0], bias.shape[0]

    def up(j):
        z = dot(wup[...], window(xs, j - 1, 3 * CB)) + bias[...]
        s = jax.nn.sigmoid(z)
        act = z * s
        slope_out[j - 1] = (s + act * (1.0 - s)).astype(BF16)
        act = act.astype(BF16)
        acts[pl.ds((j - 1) * hid, hid), :] = act
        if j in (1, 2):
            acts_out[j - 1] = act
        if j in (n - 3, n - 2):
            acts_out[j - n + 5] = act

    def down(r):
        fore_out[r - 2] = state[r] + shifted_sum(dot(wdn[...], window(acts, r - 2, hid)))

    place_row(xs, 0, own[0])
    place_row(xs, 1, own[1])
    for j in range(1, n - 1):
        place_row(xs, j + 1, own[j + 1])
        up(j)
        if j >= 3:
            down(j - 1)


def edge_forward(flags, far, near, own, inner, inner_acts, state, obs, nxt, cell, chan, wup, bias, wdn,
                 fore_out, lb_out, far_out, near_out, slope_out, acc_out, xs, acts, chans):
    n, hid = own.shape[0], bias.shape[0]
    has_low, has_high, has_next = flags[0], flags[1], flags[2]
    chans[...] = jnp.broadcast_to(chan[...], chans.shape)
    for i in range(2):
        below, above = halos(flags, far, near, i)
        place_row(xs, i, below)
        place_row(xs, 2 + i, own[i])
        place_row(xs, 4 + i, own[n - 2 + i])
        place_row(xs, 6 + i, above)
        acts[pl.ds((2 + i) * hid, hid), :] = inner_acts[i]
        acts[pl.ds((4 + i) * hid, hid), :] = inner_acts[2 + i]

    def up(x_at, act_at, slope_at, inside):
        z = dot(wup[...], window(xs, x_at, 3 * CB)) + bias[...]
        s = jax.nn.sigmoid(z)
        act = z * s
        slope = s + act * (1.0 - s)
        if inside is not None:
            act, slope = act * inside, slope * inside
        acts[pl.ds(act_at * hid, hid), :] = act.astype(BF16)
        slope_out[slope_at] = slope.astype(BF16)

    def finish(r, fore):
        st = state[r]
        fore_out[r] = fore.astype(BF16)
        w = chans[...] * cell[pl.ds(r, 1), :].astype(F32)
        lam = w * (fore - obs[r]) - has_next * (nxt[r].astype(F32) - fore)
        lb_out[r] = lam.astype(BF16)
        acc_out[r] = st - STEP * (st + lam)
        return lam

    up(0, 0, 0, has_low)
    up(1, 1, 1, None)
    up(4, 6, 2, None)
    up(5, 7, 3, has_high)
    edges = [
        finish(r, state[r] + shifted_sum(dot(wdn[...], window(acts, at, hid))))
        for r, at in ((0, 0), (1, 1), (n - 2, 4), (n - 1, 5))
    ]
    send_edges(flags, edges, far_out, near_out)
    for r in range(2, n - 2):
        finish(r, inner[r - 2])


def inner_adjoint(own, slope, wup, wdn, grad_out, rows_out, xs, grads):
    n, hid = own.shape[0], slope.shape[1]

    def up(j):
        g = (dot(wup[...], window(xs, j - 1, 3 * CB)) * slope[j - 1].astype(F32)).astype(BF16)
        grads[pl.ds((j - 1) * hid, hid), :] = g
        if j in (1, 2):
            rows_out[j - 1] = g
        if j in (n - 3, n - 2):
            rows_out[j - n + 5] = g

    def down(r):
        grad_out[r - 2] = shifted_sum(dot(wdn[...], window(grads, r - 2, hid)))

    place_row(xs, 0, own[0])
    place_row(xs, 1, own[1])
    for j in range(1, n - 1):
        place_row(xs, j + 1, own[j + 1])
        up(j)
        if j >= 3:
            down(j - 1)


def edge_adjoint(flags, far, near, own, inner, inner_rows, slope, acc, prev, ground, wup, wdn,
                 state_out, xb_out, far_out, near_out, xs, grads):
    n, hid = own.shape[0], slope.shape[1]
    first = flags[3] > 0.5
    for i in range(2):
        below, above = halos(flags, far, near, i)
        place_row(xs, i, below)
        place_row(xs, 2 + i, own[i])
        place_row(xs, 4 + i, own[n - 2 + i])
        place_row(xs, 6 + i, above)
        grads[pl.ds((2 + i) * hid, hid), :] = inner_rows[i]
        grads[pl.ds((4 + i) * hid, hid), :] = inner_rows[2 + i]

    def up(x_at, at, slope_at):
        g = dot(wup[...], window(xs, x_at, 3 * CB)) * slope[slope_at].astype(F32)
        grads[pl.ds(at * hid, hid), :] = g.astype(BF16)

    def finish(r, grad):
        earlier = jnp.where(first, ground[r], prev[r].astype(F32))
        st = acc[r] + STEP * (earlier - grad)
        state_out[r] = st
        xb_out[r] = st.astype(BF16)
        return st

    up(0, 0, 0)
    up(1, 1, 1)
    up(4, 6, 2)
    up(5, 7, 3)
    edges = [
        finish(r, shifted_sum(dot(wdn[...], window(grads, at, hid))))
        for r, at in ((0, 0), (1, 1), (n - 2, 4), (n - 1, 5))
    ]
    send_edges(flags, edges, far_out, near_out)
    for r in range(2, n - 2):
        finish(r, inner[r - 2])


def stack_out(w):
    w = jnp.pad(w, ((0, 0), (0, CF - w.shape[1]), (0, 0))).reshape(3, 3, CF, w.shape[2])
    return w.transpose(1, 2, 0, 3).reshape(3 * CF, -1)


def stack_in(w):
    w = jnp.pad(w, ((0, 0), (0, 0), (0, CB - w.shape[2])))
    return w.transpose(1, 0, 2).reshape(w.shape[1], 9 * CB)


def adjoint_taps(w):
    return jnp.flip(w, 0).transpose(0, 2, 1)


def by_rows(x):
    x = x.transpose(1, 0, 2)
    return jnp.pad(x, ((0, 0), (0, CF - x.shape[1]), (0, 0)))


def local(first_guess, background, observed, cell_mask, chan_mask, w_in, b_in, w_out):
    c, n, lon = first_guess.shape[1:]
    hid = b_in.shape[0]
    lat, lats = lax.axis_index("lat"), lax.axis_size("lat")
    tm, tms = lax.axis_index("tm"), lax.axis_size("tm")
    odd = lat % 2 == 1
    flags = jnp.stack([lat > 0, lat < lats - 1, tm < tms - 1, tm == 0, odd]).astype(F32)
    near_pairs = [p for i in range(0, lats - 1, 2) for p in ((i, i + 1), (i + 1, i))]
    far_pairs = [p for i in range(1, lats - 1, 2) for p in ((i, i + 1), (i + 1, i))]
    ahead = [(i, i + 1) for i in range(tms - 1)]
    back = [(j, i) for i, j in ahead]

    def exchange(far, near):
        return lax.ppermute(far, "lat", far_pairs), lax.ppermute(near, "lat", near_pairs)

    guess = first_guess[0]
    nxt = by_rows(lax.ppermute(guess.astype(BF16), "tm", back))
    low, high = guess[:, :2], guess[:, n - 2 :]
    far = by_rows(jnp.where(odd, high, low).astype(BF16))
    near = by_rows(jnp.where(odd, low, high).astype(BF16))
    far, near = exchange(far, near)
    state = by_rows(guess)
    xb = by_rows(guess.astype(BF16))
    obs, ground = by_rows(observed[0]), by_rows(background)
    cell = cell_mask[0]
    chan = jnp.pad(chan_mask[0].astype(F32), (0, CF - c))[:, None]
    up1, dn1 = stack_in(w_in), stack_out(w_out)
    up2, dn2 = stack_in(adjoint_taps(w_out)), stack_out(adjoint_taps(w_in))
    bias = b_in[:, None]
    S = jax.ShapeDtypeStruct
    rows_f, rows_b = S((n, CF, lon), F32), S((n, CF, lon), BF16)
    edge, mids = S((2, CF, lon), BF16), S((n - 4, CF, lon), F32)
    four, six = S((4, hid, lon), BF16), S((n - 2, hid, lon), BF16)
    unit = 2 * 9 * c * hid * lon

    def call(body, name, count, outs, scratch, rows):
        return pl.pallas_call(
            body,
            out_shape=outs,
            in_specs=([SMEM] if body in (edge_forward, edge_adjoint) else []) + [VMEM] * count,
            out_specs=(VMEM,) * len(outs),
            scratch_shapes=scratch,
            compiler_params=pltpu.CompilerParams(vmem_limit_bytes=16 * 2**20),
            cost_estimate=pl.CostEstimate(flops=rows * unit, bytes_accessed=4 * 2**20, transcendentals=0),
            name=name,
        )

    def scratch(x_rows, h_rows):
        return [pltpu.VMEM((x_rows * 3 * CB, lon), BF16), pltpu.VMEM((h_rows * hid, lon), BF16)]

    fwd_in = call(inner_forward, "inner_forward", 5, (mids, four, six), scratch(n, n - 2), 10)
    fwd_out = call(edge_forward, "edge_forward", 13, (rows_b, rows_b, edge, edge, four, rows_f),
                   scratch(8, 8) + [pltpu.VMEM((CF, lon), F32)], 8)
    adj_in = call(inner_adjoint, "inner_adjoint", 4, (mids, four), scratch(n, n - 2), 10)
    adj_out = call(edge_adjoint, "edge_adjoint", 11, (rows_f, rows_b, edge, edge), scratch(8, 8), 8)
    for step in range(ITERS):
        mid, mid_acts, slope_in = fwd_in(xb, state, up1, bias, dn1)
        fore, lb, far, near, slope_out, acc = fwd_out(
            flags, far, near, xb, mid, mid_acts, state, obs, nxt, cell, chan, up1, bias, dn1)
        prev = lax.ppermute(fore, "tm", ahead)
        far, near = exchange(far, near)
        mid, mid_rows = adj_in(lb, slope_in, up2, dn2)
        state, xb, far, near = adj_out(
            flags, far, near, lb, mid, mid_rows, slope_out, acc, prev, ground, up2, dn2)
        if step < ITERS - 1:
            nxt = lax.ppermute(xb, "tm", back)
            far, near = exchange(far, near)
    return state[:, :c].transpose(1, 0, 2)[None]


def solution(mesh):
    return jax.shard_map(
        local,
        mesh=mesh,
        in_specs=(
            P("tm", None, "lat", None),
            P(None, "lat", None),
            P("tm", None, "lat", None),
            P("tm", "lat", None),
            P("tm", None),
            P(),
            P(),
            P(),
        ),
        out_specs=P("tm", None, "lat", None),
        check_vma=False,
    )
```

profile of v0, /device:TPU:95, one launch (start us, length us, event | category | flops | bytes accessed | tf_op | source)
XLA Modules:
  0.0 96.0 jit_solution(11810401621939680179)
XLA Ops:
  0.0 1.9 %copy.84 = bf16[1,69,8,512]{3,1,2,0:T(8,128)(2,1)S(1)} copy(f32[1,69,8,512]{3,2,1,0:T(8,128)} %param.8) | data formatting | bytes 1695744 | tf_op args[0]
  2.9 2.6 %collective-permute-start.2 = (bf16[69,8,512]{2,1,0:T(8,128)(2,1)}, bf16[69,8,512]{2,1,0:T(8,128)(2,1)}, u32[]{:S(2)}, u32[]{:S(2)}) collective-permute-start(bf16[69,8,512]{2,1,0:T(8,128)(2,1)} %copy.48), channel_id=1, source_target_pairs={{8,0},{16,8},{24,16},{32,24},{40,32},{48,40},{56,48},{64,56},{72,6... | collective-permute-start | bytes 1695752 | tf_op jit(solution)/shard_map/ppermute | solution.py:222
  5.5 6.7 %collective-permute-start = (bf16[2,72,512]{2,1,0:T(8,128)(2,1)S(1)}, bf16[2,72,512]{2,1,0:T(8,128)(2,1)S(1)}, u32[]{:S(2)}, u32[]{:S(2)}) collective-permute-start(bf16[2,72,512]{2,1,0:T(8,128)(2,1)S(1)} %pad.42), channel_id=1, source_target_pairs={{1,2},{2,1},{3,4},{4,3},{5,6},{6,5},{9,10},{10,9},{11,12},{12,11},... | collective-permute-start | bytes 442376 | tf_op jit(solution)/shard_map/ppermute | solution.py:219
  12.9 1.4 %copy.85 = bf16[1,69,8,512]{3,1,2,0:T(8,128)(2,1)} copy(f32[1,69,8,512]{3,2,1,0:T(8,128)S(1)} %copy-done.7) | data formatting | bytes 1695744 | tf_op args[0]
  18.2 2.1 %inner_forward.2 = (f32[4,72,512]{2,1,0:T(8,128)S(1)}, bf16[4,128,512]{2,1,0:T(8,128)(2,1)S(1)}, bf16[6,128,512]{2,1,0:T(8,128)(2,1)S(1)}) custom-call(bf16[8,72,512]{2,1,0:T(8,128)(2,1)S(1)} %pad.44.own, f32[8,72,512]{2,1,0:T(8,128)S(1)} %pad.45.state, bf16[128,720]{1,0:T(8,128)(2,1)S(1)} %copy.45.wup, f32[128,1]{1,0:T(8,128)S(1)} %copy.46.bias, ...), custom_call_target="tpu_custom_call" | custom-call | flops 813957120 | bytes 4194304 | tf_op jit(solution)/shard_map/inner_forward/pallas_call | solution.py:262
  20.4 1.5 %copy.81 = bf16[69,8,512]{2,0,1:T(8,128)(2,1)S(1)} copy(bf16[69,8,512]{2,1,0:T(8,128)(2,1)} %collective-permute-done.2) | data formatting | bytes 1130496 | tf_op jit(solution)/shard_map/ppermute | solution.py:222
  22.0 3.3 %edge_forward.2 = (bf16[8,72,512]{2,1,0:T(8,128)(2,1)}, bf16[8,72,512]{2,1,0:T(8,128)(2,1)S(1)}, bf16[2,72,512]{2,1,0:T(8,128)(2,1)}, bf16[2,72,512]{2,1,0:T(8,1...) custom-call(f32[5]{0:T(128)S(1)} %convert_element_type.37.flags, ...), custom_call_target="tpu_custom_call" | custom-call | flops 651165696 | bytes 4194304 | tf_op jit(solution)/shard_map/edge_forward/pallas_call | solution.py:263
  25.2 5.5 %collective-permute-start.5 = (bf16[8,72,512]{2,1,0:T(8,128)(2,1)}, bf16[8,72,512]{2,1,0:T(8,128)(2,1)}, u32[]{:S(2)}, u32[]{:S(2)}) collective-permute-start(bf16[8,72,512]{2,1,0:T(8,128)(2,1)} %get-tuple-element.42), channel_id=1, source_target_pairs={{0,8},{8,16},{16,24},{24,32},{32,40},{40,48},{48,56},{56,64},{64,7... | collective-permute-start | bytes 1769480 | tf_op jit(solution)/shard_map/ppermute | solution.py:265
  30.9 4.8 %collective-permute-start.3 = (bf16[2,72,512]{2,1,0:T(8,128)(2,1)}, bf16[2,72,512]{2,1,0:T(8,128)(2,1)S(1)}, u32[]{:S(2)}, u32[]{:S(2)}) collective-permute-start(bf16[2,72,512]{2,1,0:T(8,128)(2,1)} %get-tuple-element.34), channel_id=1, source_target_pairs={{1,2},{2,1},{3,4},{4,3},{5,6},{6,5},{9,10},{10,9},{11,12},{12,11},... | collective-permute-start | bytes 442376 | tf_op jit(solution)/shard_map/ppermute | solution.py:219
  37.8 1.9 %copy.78 = f32[69,8,512]{2,0,1:T(8,128)S(1)} copy(f32[69,8,512]{2,1,0:T(8,128)} %param.9) | data formatting | bytes 2260992 | tf_op args[1]
  41.0 1.8 %inner_adjoint.2 = (f32[4,72,512]{2,1,0:T(8,128)S(1)}, bf16[4,128,512]{2,1,0:T(8,128)(2,1)S(1)}) custom-call(bf16[8,72,512]{2,1,0:T(8,128)(2,1)S(1)} %copy-done.1, bf16[6,128,512]{2,1,0:T(8,128)(2,1)S(1)} %copy-done.6, bf16[128,720]{1,0:T(8,128)(2,1)S(1)} %copy.54.wup, bf16[216,384]{1,0:T(8,128)(2,1)S(1)} %bitcast.73), custom_call_target="tpu_custom_call" | custom-call | flops 813957120 | bytes 4194304 | tf_op jit(solution)/shard_map/inner_adjoint/pallas_call | solution.py:267
  42.8 4.6 %collective-permute-done.3.far = bf16[2,72,512]{2,1,0:T(8,128)(2,1)S(1)} collective-permute-done((bf16[2,72,512]{2,1,0:T(8,128)(2,1)}, bf16[2,72,512]{2,1,0:T(8,128)(2,1)S(1)}, u32[]{:S(2)}, u32[]{:S(2)}) %collective-permute-start.3) | collective-permute-done | bytes 147488 | tf_op jit(solution)/shard_map/ppermute | solution.py:219
  47.4 2.5 %edge_adjoint.2 = (f32[8,72,512]{2,1,0:T(8,128)S(1)}, bf16[8,72,512]{2,1,0:T(8,128)(2,1)S(1)}, bf16[2,72,512]{2,1,0:T(8,128)(2,1)S(1)}, bf16[2,72,512]{2,1,0:T(8,128)(2,1)S(1)}) custom-call(f32[5]{0:T(128)S(1)} %convert_element_type.37.flags, bf16[2,72,512]{2,1,0:T(8,128)(2,1)S(1)} %collective-permute-done.3.far, ...), custom_call_target="tpu_custom_call" | custom-call | flops 651165696 | bytes 4194304 | tf_op jit(solution)/shard_map/edge_adjoint/pallas_call | solution.py:268
  49.9 1.9 %collective-permute-start.8 = (bf16[8,72,512]{2,1,0:T(8,128)(2,1)S(1)}, bf16[8,72,512]{2,1,0:T(8,128)(2,1)S(1)}, u32[]{:S(2)}, u32[]{:S(2)}) collective-permute-start(bf16[8,72,512]{2,1,0:T(8,128)(2,1)S(1)} %get-tuple-element.45.own), channel_id=1, source_target_pairs={{8,0},{16,8},{24,16},{32,24},{40,32},{48,40},{56,48},{64,56},{72,6... | collective-permute-start | bytes 1769480 | tf_op jit(solution)/shard_map/ppermute | solution.py:271
  51.9 4.9 %collective-permute-start.6 = (bf16[2,72,512]{2,1,0:T(8,128)(2,1)S(1)}, bf16[2,72,512]{2,1,0:T(8,128)(2,1)S(1)}, u32[]{:S(2)}, u32[]{:S(2)}) collective-permute-start(bf16[2,72,512]{2,1,0:T(8,128)(2,1)S(1)} %get-tuple-element.43), channel_id=1, source_target_pairs={{1,2},{2,1},{3,4},{4,3},{5,6},{6,5},{9,10},{10,9},{11,12},{12,11},... | collective-permute-start | bytes 442376 | tf_op jit(solution)/shard_map/ppermute | solution.py:219
  56.9 2.1 %inner_forward.3 = (f32[4,72,512]{2,1,0:T(8,128)S(1)}, bf16[4,128,512]{2,1,0:T(8,128)(2,1)S(1)}, bf16[6,128,512]{2,1,0:T(8,128)(2,1)S(1)}) custom-call(bf16[8,72,512]{2,1,0:T(8,128)(2,1)S(1)} %get-tuple-element.45.own, f32[8,72,512]{2,1,0:T(8,128)S(1)} %get-tuple-element.46.state, bf16[128,720]{1,0:T(8,128)(2,1)S(1)} %copy.45.wup, f32[128,1]{1,0:T(8,128)S(1)} %copy.46.bias, ...), custom_call_target="tpu_custom_call" | custom-call | flops 813957120 | bytes 4194304 | tf_op jit(solution)/shard_map/inner_forward/pallas_call | solution.py:262
  59.0 7.1 %collective-permute-done.6.far = bf16[2,72,512]{2,1,0:T(8,128)(2,1)S(1)} collective-permute-done((bf16[2,72,512]{2,1,0:T(8,128)(2,1)S(1)}, bf16[2,72,512]{2,1,0:T(8,128)(2,1)S(1)}, u32[]{:S(2)}, u32[]{:S(2)}) %collective-permute-start.6) | collective-permute-done | bytes 147488 | tf_op jit(solution)/shard_map/ppermute | solution.py:219
  66.2 2.4 %edge_forward.3 = (bf16[8,72,512]{2,1,0:T(8,128)(2,1)S(1)}, bf16[8,72,512]{2,1,0:T(8,128)(2,1)S(1)}, bf16[2,72,512]{2,1,0:T(8,128)(2,1)S(1)}, bf16[2,72,512]{2,1...) custom-call(f32[5]{0:T(128)S(1)} %convert_element_type.37.flags, ...), custom_call_target="tpu_custom_call" | custom-call | flops 651165696 | bytes 4194304 | tf_op jit(solution)/shard_map/edge_forward/pallas_call | solution.py:263
  68.5 5.9 %collective-permute-start.11 = (bf16[8,72,512]{2,1,0:T(8,128)(2,1)S(1)}, bf16[8,72,512]{2,1,0:T(8,128)(2,1)S(1)}, u32[]{:S(2)}, u32[]{:S(2)}) collective-permute-start(bf16[8,72,512]{2,1,0:T(8,128)(2,1)S(1)} %get-tuple-element.57), channel_id=1, source_target_pairs={{0,8},{8,16},{16,24},{24,32},{32,40},{40,48},{48,56},{56,64},{64,7... | collective-permute-start | bytes 1769480 | tf_op jit(solution)/shard_map/ppermute | solution.py:265
  74.4 5.4 %collective-permute-start.9 = (bf16[2,72,512]{2,1,0:T(8,128)(2,1)S(1)}, bf16[2,72,512]{2,1,0:T(8,128)(2,1)S(1)}, u32[]{:S(2)}, u32[]{:S(2)}) collective-permute-start(bf16[2,72,512]{2,1,0:T(8,128)(2,1)S(1)} %get-tuple-element.49), channel_id=1, source_target_pairs={{1,2},{2,1},{3,4},{4,3},{5,6},{6,5},{9,10},{10,9},{11,12},{12,11},... | collective-permute-start | bytes 442376 | tf_op jit(solution)/shard_map/ppermute | solution.py:219
  80.1 1.8 %inner_adjoint.3 = (f32[4,72,512]{2,1,0:T(8,128)S(1)}, bf16[4,128,512]{2,1,0:T(8,128)(2,1)S(1)}) custom-call(bf16[8,72,512]{2,1,0:T(8,128)(2,1)S(1)} %get-tuple-element.51.own, bf16[6,128,512]{2,1,0:T(8,128)(2,1)S(1)} %get-tuple-element.52.slope, bf16[128,720]{1,0:T(8,128)(2,1)S(1)} %copy.54.wup, bf16[216,384]{1,0:T(8,128)(2,1)S(1)} %bitcast.75), custom_call_target="tpu_custom_call" | custom-call | flops 813957120 | bytes 4194304 | tf_op jit(solution)/shard_map/inner_adjoint/pallas_call | solution.py:267
  81.9 9.6 %collective-permute-done.9.far = bf16[2,72,512]{2,1,0:T(8,128)(2,1)S(1)} collective-permute-done((bf16[2,72,512]{2,1,0:T(8,128)(2,1)S(1)}, bf16[2,72,512]{2,1,0:T(8,128)(2,1)S(1)}, u32[]{:S(2)}, u32[]{:S(2)}) %collective-permute-start.9) | collective-permute-done | bytes 147488 | tf_op jit(solution)/shard_map/ppermute | solution.py:219
  91.5 2.8 %edge_adjoint.3 = (f32[8,72,512]{2,1,0:T(8,128)S(1)}, bf16[8,72,512]{2,1,0:T(8,128)(2,1)}, bf16[2,72,512]{2,1,0:T(8,128)(2,1)}, bf16[2,72,512]{2,1,0:T(8,128)(2,1)}) custom-call(f32[5]{0:T(128)S(1)} %convert_element_type.37.flags, bf16[2,72,512]{2,1,0:T(8,128)(2,1)S(1)} %collective-permute-done.9.far, bf16[2,72,512]{2,1,0:T(8,128)(2,1)S(1)} %collective-permute-done.10.near, ...), custom_call_target="tpu_custom_call" | custom-call | flops 651165696 | bytes 4194304 | tf_op jit(solution)/shard_map/edge_adjoint/pallas_call | solution.py:268
  94.4 1.7 %copy.64 = f32[1,69,8,512]{3,2,1,0:T(8,128)} copy(f32[1,69,8,512]{3,1,2,0:T(8,128)S(1)} %slice_bitcast_fusion) | data formatting | bytes 2260992 | tf_op jit(solution)/shard_map/broadcast_in_dim | solution.py:273
  (73 shorter events, 9.6 us)
Async XLA Ops:
  1.9 11.0 %copy-start.7 = (f32[1,69,8,512]{3,2,1,0:T(8,128)S(1)}, f32[1,69,8,512]{3,2,1,0:T(8,128)}, u32[]{:S(2)}) copy-start(f32[1,69,8,512]{3,2,1,0:T(8,128)} %param.8) | copy-start | bytes 3391492
  2.9 17.5 %collective-permute-start.2 = (bf16[69,8,512]{2,1,0:T(8,128)(2,1)}, bf16[69,8,512]{2,1,0:T(8,128)(2,1)}, u32[]{:S(2)}, u32[]{:S(2)}) collective-permute-start(bf16[69,8,512]{2,1,0:T(8,128)(2,1)} %copy.48), channel_id=1, source_target_pairs={{8,0},{16,8},{24,16},{32,24},{40,32},{48,40},{56,48},{64,56},{72,6... | collective-permute-start | bytes 1695752 | tf_op jit(solution)/shard_map/ppermute | solution.py:222
  5.5 16.4 %collective-permute-start = (bf16[2,72,512]{2,1,0:T(8,128)(2,1)S(1)}, bf16[2,72,512]{2,1,0:T(8,128)(2,1)S(1)}, u32[]{:S(2)}, u32[]{:S(2)}) collective-permute-start(bf16[2,72,512]{2,1,0:T(8,128)(2,1)S(1)} %pad.42), channel_id=1, source_target_pairs={{1,2},{2,1},{3,4},{4,3},{5,6},{6,5},{9,10},{10,9},{11,12},{12,11},... | collective-permute-start | bytes 442376 | tf_op jit(solution)/shard_map/ppermute | solution.py:219
  12.9 9.1 %collective-permute-start.1 = (bf16[2,72,512]{2,1,0:T(8,128)(2,1)}, bf16[2,72,512]{2,1,0:T(8,128)(2,1)S(1)}, u32[]{:S(2)}, u32[]{:S(2)}) collective-permute-start(bf16[2,72,512]{2,1,0:T(8,128)(2,1)} %pad.43), channel_id=1, source_target_pairs={{0,1},{1,0},{2,3},{3,2},{4,5},{5,4},{6,7},{7,6},{8,9},{9,8},{10,11... | collective-permute-start | bytes 442376 | tf_op jit(solution)/shard_map/ppermute | solution.py:219
  14.3 1.0 %copy-start.10 = (bf16[9,69,128]{2,1,0:T(8,128)(2,1)S(1)}, bf16[9,69,128]{2,1,0:T(8,128)(2,1)}, u32[]{:S(2)}) copy-start(bf16[9,69,128]{2,1,0:T(8,128)(2,1)} %param.15) | copy-start | bytes 476932
  15.0 1.2 %copy-start.8 = (bf16[1,69,8,512]{3,1,2,0:T(8,128)(2,1)S(1)}, bf16[1,69,8,512]{3,1,2,0:T(8,128)(2,1)}, u32[]{:S(2)}) copy-start(bf16[1,69,8,512]{3,1,2,0:T(8,128)(2,1)} %copy.85) | copy-start | bytes 1695748
  16.1 1.3 %copy-start.9 = (f32[1,69,8,512]{3,2,1,0:T(8,128)S(1)}, f32[1,69,8,512]{3,2,1,0:T(8,128)}, u32[]{:S(2)}) copy-start(f32[1,69,8,512]{3,2,1,0:T(8,128)} %param.10) | copy-start | bytes 3391492
  20.3 1.6 %copy-start.5 = (bf16[6,128,512]{2,1,0:T(8,128)(2,1)}, bf16[6,128,512]{2,1,0:T(8,128)(2,1)S(1)}, u32[]{:S(2)}) copy-start(bf16[6,128,512]{2,1,0:T(8,128)(2,1)S(1)} %get-tuple-element.37.slope) | copy-start | bytes 2359300
  20.3 1.6 %copy-start.4 = (s32[1,8,512]{2,1,0:T(8,128)S(1)}, s32[1,8,512]{2,1,0:T(8,128)}, u32[]{:S(2)}) copy-start(s32[1,8,512]{2,1,0:T(8,128)} %param.11) | copy-start | bytes 49156
  25.2 11.5 %copy-start = (bf16[8,72,512]{2,1,0:T(8,128)(2,1)}, bf16[8,72,512]{2,1,0:T(8,128)(2,1)S(1)}, u32[]{:S(2)}) copy-start(bf16[8,72,512]{2,1,0:T(8,128)(2,1)S(1)} %get-tuple-element.36.own) | copy-start | bytes 1769476
  25.2 11.5 %copy-start.2 = (bf16[4,128,512]{2,1,0:T(8,128)(2,1)}, bf16[4,128,512]{2,1,0:T(8,128)(2,1)S(1)}, u32[]{:S(2)}) copy-start(bf16[4,128,512]{2,1,0:T(8,128)(2,1)S(1)} %get-tuple-element.40.slope) | copy-start | bytes 1572868
  25.2 10.7 %copy-start.11 = (bf16[9,69,128]{2,1,0:T(8,128)(2,1)S(1)}, bf16[9,69,128]{2,1,0:T(8,128)(2,1)}, u32[]{:S(2)}) copy-start(bf16[9,69,128]{2,1,0:T(8,128)(2,1)} %param.15) | copy-start | bytes 476932
  25.2 22.1 %collective-permute-start.5 = (bf16[8,72,512]{2,1,0:T(8,128)(2,1)}, bf16[8,72,512]{2,1,0:T(8,128)(2,1)}, u32[]{:S(2)}, u32[]{:S(2)}) collective-permute-start(bf16[8,72,512]{2,1,0:T(8,128)(2,1)} %get-tuple-element.42), channel_id=1, source_target_pairs={{0,8},{8,16},{16,24},{24,32},{32,40},{40,48},{48,56},{56,64},{64,7... | collective-permute-start | bytes 1769480 | tf_op jit(solution)/shard_map/ppermute | solution.py:265
  30.9 16.5 %collective-permute-start.3 = (bf16[2,72,512]{2,1,0:T(8,128)(2,1)}, bf16[2,72,512]{2,1,0:T(8,128)(2,1)S(1)}, u32[]{:S(2)}, u32[]{:S(2)}) collective-permute-start(bf16[2,72,512]{2,1,0:T(8,128)(2,1)} %get-tuple-element.34), channel_id=1, source_target_pairs={{1,2},{2,1},{3,4},{4,3},{5,6},{6,5},{9,10},{10,9},{11,12},{12,11},... | collective-permute-start | bytes 442376 | tf_op jit(solution)/shard_map/ppermute | solution.py:219
  35.7 11.7 %collective-permute-start.4 = (bf16[2,72,512]{2,1,0:T(8,128)(2,1)}, bf16[2,72,512]{2,1,0:T(8,128)(2,1)S(1)}, u32[]{:S(2)}, u32[]{:S(2)}) collective-permute-start(bf16[2,72,512]{2,1,0:T(8,128)(2,1)} %get-tuple-element.35), channel_id=1, source_target_pairs={{0,1},{1,0},{2,3},{3,2},{4,5},{5,4},{6,7},{7,6},{8,9},{9,8},{10,11... | collective-permute-start | bytes 442376 | tf_op jit(solution)/shard_map/ppermute | solution.py:219
  39.7 1.1 %copy-start.1 = (bf16[8,72,512]{2,1,0:T(8,128)(2,1)S(1)}, bf16[8,72,512]{2,1,0:T(8,128)(2,1)}, u32[]{:S(2)}) copy-start(bf16[8,72,512]{2,1,0:T(8,128)(2,1)} %copy-done) | copy-start | bytes 1769476
  39.7 1.3 %copy-start.6 = (bf16[6,128,512]{2,1,0:T(8,128)(2,1)S(1)}, bf16[6,128,512]{2,1,0:T(8,128)(2,1)}, u32[]{:S(2)}) copy-start(bf16[6,128,512]{2,1,0:T(8,128)(2,1)} %copy-done.5) | copy-start | bytes 2359300
  41.0 6.4 %copy-start.3 = (bf16[4,128,512]{2,1,0:T(8,128)(2,1)S(1)}, bf16[4,128,512]{2,1,0:T(8,128)(2,1)}, u32[]{:S(2)}) copy-start(bf16[4,128,512]{2,1,0:T(8,128)(2,1)} %copy-done.2) | copy-start | bytes 1572868
  49.9 16.2 %collective-permute-start.8 = (bf16[8,72,512]{2,1,0:T(8,128)(2,1)S(1)}, bf16[8,72,512]{2,1,0:T(8,128)(2,1)S(1)}, u32[]{:S(2)}, u32[]{:S(2)}) collective-permute-start(bf16[8,72,512]{2,1,0:T(8,128)(2,1)S(1)} %get-tuple-element.45.own), channel_id=1, source_target_pairs={{8,0},{16,8},{24,16},{32,24},{40,32},{48,40},{56,48},{64,56},{72,6... | collective-permute-start | bytes 1769480 | tf_op jit(solution)/shard_map/ppermute | solution.py:271
  51.9 14.3 %collective-permute-start.6 = (bf16[2,72,512]{2,1,0:T(8,128)(2,1)S(1)}, bf16[2,72,512]{2,1,0:T(8,128)(2,1)S(1)}, u32[]{:S(2)}, u32[]{:S(2)}) collective-permute-start(bf16[2,72,512]{2,1,0:T(8,128)(2,1)S(1)} %get-tuple-element.43), channel_id=1, source_target_pairs={{1,2},{2,1},{3,4},{4,3},{5,6},{6,5},{9,10},{10,9},{11,12},{12,11},... | collective-permute-start | bytes 442376 | tf_op jit(solution)/shard_map/ppermute | solution.py:219
  56.8 9.4 %collective-permute-start.7 = (bf16[2,72,512]{2,1,0:T(8,128)(2,1)S(1)}, bf16[2,72,512]{2,1,0:T(8,128)(2,1)S(1)}, u32[]{:S(2)}, u32[]{:S(2)}) collective-permute-start(bf16[2,72,512]{2,1,0:T(8,128)(2,1)S(1)} %get-tuple-element.44), channel_id=1, source_target_pairs={{0,1},{1,0},{2,3},{3,2},{4,5},{5,4},{6,7},{7,6},{8,9},{9,8},{10,11... | collective-permute-start | bytes 442376 | tf_op jit(solution)/shard_map/ppermute | solution.py:219
  68.5 22.9 %collective-permute-start.11 = (bf16[8,72,512]{2,1,0:T(8,128)(2,1)S(1)}, bf16[8,72,512]{2,1,0:T(8,128)(2,1)S(1)}, u32[]{:S(2)}, u32[]{:S(2)}) collective-permute-start(bf16[8,72,512]{2,1,0:T(8,128)(2,1)S(1)} %get-tuple-element.57), channel_id=1, source_target_pairs={{0,8},{8,16},{16,24},{24,32},{32,40},{40,48},{48,56},{56,64},{64,7... | collective-permute-start | bytes 1769480 | tf_op jit(solution)/shard_map/ppermute | solution.py:265
  74.4 17.0 %collective-permute-start.9 = (bf16[2,72,512]{2,1,0:T(8,128)(2,1)S(1)}, bf16[2,72,512]{2,1,0:T(8,128)(2,1)S(1)}, u32[]{:S(2)}, u32[]{:S(2)}) collective-permute-start(bf16[2,72,512]{2,1,0:T(8,128)(2,1)S(1)} %get-tuple-element.49), channel_id=1, source_target_pairs={{1,2},{2,1},{3,4},{4,3},{5,6},{6,5},{9,10},{10,9},{11,12},{12,11},... | collective-permute-start | bytes 442376 | tf_op jit(solution)/shard_map/ppermute | solution.py:219
  79.8 11.7 %collective-permute-start.10 = (bf16[2,72,512]{2,1,0:T(8,128)(2,1)S(1)}, bf16[2,72,512]{2,1,0:T(8,128)(2,1)S(1)}, u32[]{:S(2)}, u32[]{:S(2)}) collective-permute-start(bf16[2,72,512]{2,1,0:T(8,128)(2,1)S(1)} %get-tuple-element.50), channel_id=1, source_target_pairs={{0,1},{1,0},{2,3},{3,2},{4,5},{5,4},{6,7},{7,6},{8,9},{9,8},{10,11... | collective-permute-start | bytes 442376 | tf_op jit(solution)/shard_map/ppermute | solution.py:219
  (3 other events, 2.7 us)
where the time goes:
time: 97.2 us; the launch traced here: 96 us
  starting transfers between devices  38.3 us (39%)
  waiting for transfers between devices  21.3 us (22%)
  Pallas kernels  18.7 us (19%)
  local copies, waits for them, and re-layouts  17.2 us (18%)
    ppermute x4, starting transfers between devices, exchange(): lax.ppermute(far, 'lat', far_pairs)  21.8 us
    ppermute x4, waiting for transfers between devices, exchange(): lax.ppermute(far, 'lat', far_pairs)  21.3 us
    ppermute x2, starting transfers between devices, local(): prev = lax.ppermute(fore, 'tm', ahead)  11.3 us
    unnamed x37, local copies, waits for them, and re-layouts  9.42 us
    pallas_call x2, Pallas kernels, local(): fwd_out(flags, far, near, xb, mid, mid_acts, state, obs, nxt, cell, chan,...  5.66 us
    pallas_call x2, Pallas kernels, local(): adj_out(flags, far, near, lb, mid, mid_rows, slope_out, acc, prev, ground...  5.36 us
    pallas_call x2, Pallas kernels, local(): mid, mid_acts, slope_in = fwd_in(xb, state, up1, bias, dn1)  4.21 us
    pallas_call x2, Pallas kernels, local(): mid, mid_rows = adj_in(lb, slope_in, up2, dn2)  3.52 us
  transfers between devices with their start and end apart: 12, of which 3 were waited for; matrix products, arithmetic and copies ran while one was open for 10% of the time, Pallas kernels for 8%

commit v1 on v0

--- a/solution.py
+++ b/solution.py
@@ -1,9 +1,12 @@
+import functools
+
 import jax
 import jax.numpy as jnp
 from jax import lax
 from jax.experimental import pallas as pl
 from jax.experimental.pallas import tpu as pltpu
 from jax.sharding import PartitionSpec as P
+
 
 ITERS = 2
 STEP = 0.25
@@ -55,7 +58,7 @@
     n, hid = own.shape[0], bias.shape[0]
 
     def up(j):
-        z = dot(wup[...], window(xs, j - 1, 3 * CB)) + bias[...]
+        z = dot(wup[...], window(xs, j - 1, 3 * CB)) + wide(bias, own.shape[2])
         s = jax.nn.sigmoid(z)
         act = z * s
         slope_out[j - 1] = (s + act * (1.0 - s)).astype(BF16)
@@ -78,11 +81,65 @@
             down(j - 1)
 
 
-def edge_forward(flags, far, near, own, inner, inner_acts, state, obs, nxt, cell, chan, wup, bias, wdn,
-                 fore_out, lb_out, far_out, near_out, slope_out, acc_out, xs, acts, chans):
+def column(row, size):
+    m = row.shape[1]
+    at = lax.broadcasted_iota(jnp.int32, (size, m), 0) == lax.broadcasted_iota(jnp.int32, (size, m), 1)
+    return jnp.sum(jnp.where(at, row, 0.0), axis=1, keepdims=True)
+
+
+def padded(v, size):
+    return jnp.concatenate([v, jnp.zeros((size - v.shape[0], v.shape[1]), F32)], axis=0)
+
+
+def prepare(flags, guess, b_row, chan_row, state_out, xb_out, far_out, near_out, bias_out, chan_out):
+    n = guess.shape[1]
+    rows = {}
+    for r in (0, 1, n - 2, n - 1, *range(2, n - 2)):
+        rows[r] = padded(guess[:, r, :], CF)
+        state_out[r] = rows[r]
+        xb_out[r] = rows[r].astype(BF16)
+    send_edges(flags, [rows[r] for r in (0, 1, n - 2, n - 1)], far_out, near_out)
+    bias_out[...] = jnp.broadcast_to(column(b_row[...], bias_out.shape[0]), bias_out.shape)
+    chan_out[...] = jnp.broadcast_to(column(chan_row[...].astype(F32), CF), chan_out.shape)
+
+
+def stack_in(taps, out):
+    width = out.shape[1]
+    whole = padded(jnp.concatenate([padded(t, CB) for t in taps], axis=0), -(-width // 128) * 128)
+    for at in range(0, width, 128):
+        size = min(128, width - at)
+        out[:, at : at + size] = whole[at : at + 128].T[:, :size].astype(BF16)
+
+
+def stack_out(taps, out):
+    hid = taps[0].shape[1]
+    for dr in range(3):
+        rows = jnp.concatenate([padded(t, CF) for t in taps[3 * dr : 3 * dr + 3]], axis=0)
+        out[:, dr * hid : (dr + 1) * hid] = rows.astype(BF16)
+
+
+def prepare_forward(w_in, w_out, field, up_out, down_out, rows_out):
+    stack_in([w_in[t].astype(F32).T for t in range(9)], up_out)
+    stack_out([w_out[t].astype(F32) for t in range(9)], down_out)
+    for r in range(field.shape[1]):
+        rows_out[r] = padded(field[:, r, :], CF)
+
+
+def prepare_adjoint(w_in, w_out, field, up_out, down_out, rows_out):
+    stack_in([w_out[8 - t].astype(F32) for t in range(9)], up_out)
+    stack_out([w_in[8 - t].astype(F32).T for t in range(9)], down_out)
+    for r in range(field.shape[1]):
+        rows_out[r] = padded(field[:, r, :], CF)
+
+
+def wide(bias, lon):
+    return jnp.concatenate([bias[...]] * (lon // bias.shape[1]), axis=1)
+
+
+def edge_forward(flags, far, near, own, inner, inner_acts, state, wup, bias, wdn,
+                 fore_out, edges_out, slope_out, xs, acts):
     n, hid = own.shape[0], bias.shape[0]
-    has_low, has_high, has_next = flags[0], flags[1], flags[2]
-    chans[...] = jnp.broadcast_to(chan[...], chans.shape)
+    has_low, has_high = flags[0], flags[1]
     for i in range(2):
         below, above = halos(flags, far, near, i)
         place_row(xs, i, below)
@@ -93,7 +150,7 @@
         acts[pl.ds((4 + i) * hid, hid), :] = inner_acts[2 + i]
 
     def up(x_at, act_at, slope_at, inside):
-        z = dot(wup[...], window(xs, x_at, 3 * CB)) + bias[...]
+        z = dot(wup[...], window(xs, x_at, 3 * CB)) + wide(bias, own.shape[2])
         s = jax.nn.sigmoid(z)
         act = z * s
         slope = s + act * (1.0 - s)
@@ -102,23 +159,31 @@
         acts[pl.ds(act_at * hid, hid), :] = act.astype(BF16)
         slope_out[slope_at] = slope.astype(BF16)
 
+    up(0, 0, 0, has_low)
+    up(1, 1, 1, None)
+    up(4, 6, 2, None)
+    up(5, 7, 3, has_high)
+    for i, (r, at) in enumerate(((0, 0), (1, 1), (n - 2, 4), (n - 1, 5))):
+        fore = state[r] + shifted_sum(dot(wdn[...], window(acts, at, hid)))
+        edges_out[i] = fore
+        fore_out[r] = fore.astype(BF16)
+    for r in range(2, n - 2):
+        fore_out[r] = inner[r - 2].astype(BF16)
+
+
+def misfit(flags, inner, outer, state, obs, nxt, cell, chan, lb_out, far_out, near_out, acc_out):
+    n = state.shape[0]
+    has_next = flags[2]
+
     def finish(r, fore):
         st = state[r]
-        fore_out[r] = fore.astype(BF16)
-        w = chans[...] * cell[pl.ds(r, 1), :].astype(F32)
+        w = chan[...] * cell[pl.ds(r, 1), :].astype(F32)
         lam = w * (fore - obs[r]) - has_next * (nxt[r].astype(F32) - fore)
         lb_out[r] = lam.astype(BF16)
         acc_out[r] = st - STEP * (st + lam)
         return lam
 
-    up(0, 0, 0, has_low)
-    up(1, 1, 1, None)
-    up(4, 6, 2, None)
-    up(5, 7, 3, has_high)
-    edges = [
-        finish(r, state[r] + shifted_sum(dot(wdn[...], window(acts, at, hid))))
-        for r, at in ((0, 0), (1, 1), (n - 2, 4), (n - 1, 5))
-    ]
+    edges = [finish(r, outer[i]) for i, r in enumerate((0, 1, n - 2, n - 1))]
     send_edges(flags, edges, far_out, near_out)
     for r in range(2, n - 2):
         finish(r, inner[r - 2])
@@ -147,8 +212,8 @@
             down(j - 1)
 
 
-def edge_adjoint(flags, far, near, own, inner, inner_rows, slope, acc, prev, ground, wup, wdn,
-                 state_out, xb_out, far_out, near_out, xs, grads):
+def edge_adjoint(last, flags, far, near, own, inner, inner_rows, slope, acc, prev, ground, wup, wdn, *refs):
+    outs, (xs, grads) = refs[:-2], refs[-2:]
     n, hid = own.shape[0], slope.shape[1]
     first = flags[3] > 0.5
     for i in range(2):
@@ -167,8 +232,11 @@
     def finish(r, grad):
         earlier = jnp.where(first, ground[r], prev[r].astype(F32))
         st = acc[r] + STEP * (earlier - grad)
-        state_out[r] = st
-        xb_out[r] = st.astype(BF16)
+        if last:
+            outs[0][:, r, :] = st[: outs[0].shape[0]]
+        else:
+            outs[0][r] = st
+            outs[1][r] = st.astype(BF16)
         return st
 
     up(0, 0, 0)
@@ -179,28 +247,10 @@
         finish(r, shifted_sum(dot(wdn[...], window(grads, at, hid))))
         for r, at in ((0, 0), (1, 1), (n - 2, 4), (n - 1, 5))
     ]
-    send_edges(flags, edges, far_out, near_out)
+    if not last:
+        send_edges(flags, edges, outs[2], outs[3])
     for r in range(2, n - 2):
         finish(r, inner[r - 2])
-
-
-def stack_out(w):
-    w = jnp.pad(w, ((0, 0), (0, CF - w.shape[1]), (0, 0))).reshape(3, 3, CF, w.shape[2])
-    return w.transpose(1, 2, 0, 3).reshape(3 * CF, -1)
-
-
-def stack_in(w):
-    w = jnp.pad(w, ((0, 0), (0, 0), (0, CB - w.shape[2])))
-    return w.transpose(1, 0, 2).reshape(w.shape[1], 9 * CB)
-
-
-def adjoint_taps(w):
-    return jnp.flip(w, 0).transpose(0, 2, 1)
-
-
-def by_rows(x):
-    x = x.transpose(1, 0, 2)
-    return jnp.pad(x, ((0, 0), (0, CF - x.shape[1]), (0, 0)))
 
 
 def local(first_guess, background, observed, cell_mask, chan_mask, w_in, b_in, w_out):
@@ -216,61 +266,64 @@
     back = [(j, i) for i, j in ahead]
 
     def exchange(far, near):
-        return lax.ppermute(far, "lat", far_pairs), lax.ppermute(near, "lat", near_pairs)
-
-    guess = first_guess[0]
-    nxt = by_rows(lax.ppermute(guess.astype(BF16), "tm", back))
-    low, high = guess[:, :2], guess[:, n - 2 :]
-    far = by_rows(jnp.where(odd, high, low).astype(BF16))
-    near = by_rows(jnp.where(odd, low, high).astype(BF16))
-    far, near = exchange(far, near)
-    state = by_rows(guess)
-    xb = by_rows(guess.astype(BF16))
-    obs, ground = by_rows(observed[0]), by_rows(background)
+        far = lax.ppermute(far, "lat", far_pairs)
+        near = lax.ppermute(near, "lat", near_pairs)
+        return far, near
+
+    def shift(x, pairs):
+        return lax.ppermute(x, "tm", pairs)
+
     cell = cell_mask[0]
-    chan = jnp.pad(chan_mask[0].astype(F32), (0, CF - c))[:, None]
-    up1, dn1 = stack_in(w_in), stack_out(w_out)
-    up2, dn2 = stack_in(adjoint_taps(w_out)), stack_out(adjoint_taps(w_in))
-    bias = b_in[:, None]
     S = jax.ShapeDtypeStruct
     rows_f, rows_b = S((n, CF, lon), F32), S((n, CF, lon), BF16)
     edge, mids = S((2, CF, lon), BF16), S((n - 4, CF, lon), F32)
     four, six = S((4, hid, lon), BF16), S((n - 2, hid, lon), BF16)
     unit = 2 * 9 * c * hid * lon
 
-    def call(body, name, count, outs, scratch, rows):
+    def call(body, count, outs, scratch, rows, flagged=True):
         return pl.pallas_call(
             body,
             out_shape=outs,
-            in_specs=([SMEM] if body in (edge_forward, edge_adjoint) else []) + [VMEM] * count,
+            in_specs=[SMEM] * flagged + [VMEM] * count,
             out_specs=(VMEM,) * len(outs),
             scratch_shapes=scratch,
             compiler_params=pltpu.CompilerParams(vmem_limit_bytes=16 * 2**20),
             cost_estimate=pl.CostEstimate(flops=rows * unit, bytes_accessed=4 * 2**20, transcendentals=0),
-            name=name,
         )
 
     def scratch(x_rows, h_rows):
         return [pltpu.VMEM((x_rows * 3 * CB, lon), BF16), pltpu.VMEM((h_rows * hid, lon), BF16)]
 
-    fwd_in = call(inner_forward, "inner_forward", 5, (mids, four, six), scratch(n, n - 2), 10)
-    fwd_out = call(edge_forward, "edge_forward", 13, (rows_b, rows_b, edge, edge, four, rows_f),
-                   scratch(8, 8) + [pltpu.VMEM((CF, lon), F32)], 8)
-    adj_in = call(inner_adjoint, "inner_adjoint", 4, (mids, four), scratch(n, n - 2), 10)
-    adj_out = call(edge_adjoint, "edge_adjoint", 11, (rows_f, rows_b, edge, edge), scratch(8, 8), 8)
+    ups, downs = S((hid, 9 * CB), BF16), S((3 * CF, 3 * hid), BF16)
+    prep = call(prepare, 3, (rows_f, rows_b, edge, edge, S((hid, 128), F32), S((CF, lon), F32)), [], 0)
+    prep_fwd = call(prepare_forward, 3, (ups, downs, rows_f), [], 4, False)
+    prep_adj = call(prepare_adjoint, 3, (ups, downs, rows_f), [], 4, False)
+    fwd_in = call(inner_forward, 5, (mids, four, six), scratch(n, n - 2), 10, False)
+    fwd_out = call(edge_forward, 9, (rows_b, mids, four), scratch(8, 8), 8)
+    fit = call(misfit, 7, (rows_b, edge, edge, rows_f), [], 0)
+    adj_in = call(inner_adjoint, 4, (mids, four), scratch(n, n - 2), 10, False)
+    adj_out = call(functools.partial(edge_adjoint, False), 11, (rows_f, rows_b, edge, edge), scratch(8, 8), 8)
+    adj_end = call(functools.partial(edge_adjoint, True), 11, (S((c, n, lon), F32),), scratch(8, 8), 8)
+    state, xb, far, near, bias, chan = prep(flags, first_guess[0], b_in[None], chan_mask)
     for step in range(ITERS):
+        far, near = exchange(far, near)
+        nxt = shift(xb, back)
+        if step == 0:
+            up1, dn1, obs = prep_fwd(w_in, w_out, observed[0])
         mid, mid_acts, slope_in = fwd_in(xb, state, up1, bias, dn1)
-        fore, lb, far, near, slope_out, acc = fwd_out(
-            flags, far, near, xb, mid, mid_acts, state, obs, nxt, cell, chan, up1, bias, dn1)
-        prev = lax.ppermute(fore, "tm", ahead)
+        fore, outer, slope_out = fwd_out(flags, far, near, xb, mid, mid_acts, state, up1, bias, dn1)
+        prev = shift(fore, ahead)
+        lb, far, near, acc = fit(flags, mid, outer, state, obs, nxt, cell, chan)
         far, near = exchange(far, near)
+        if step == 0:
+            up2, dn2, ground = prep_adj(w_in, w_out, background)
         mid, mid_rows = adj_in(lb, slope_in, up2, dn2)
-        state, xb, far, near = adj_out(
-            flags, far, near, lb, mid, mid_rows, slope_out, acc, prev, ground, up2, dn2)
+        tail = (flags, far, near, lb, mid, mid_rows, slope_out, acc, prev, ground, up2, dn2)
         if step < ITERS - 1:
-            nxt = lax.ppermute(xb, "tm", back)
-            far, near = exchange(far, near)
-    return state[:, :c].transpose(1, 0, 2)[None]
+            state, xb, far, near = adj_out(*tail)
+        else:
+            (analysis,) = adj_end(*tail)
+    return analysis[None]
 
 
 def solution(mesh):

time: 97.2 us -> 86.7 us (0.89)
  local copies, waits for them, and re-layouts: 17.2 us -> 4.86 us
  Pallas kernels: 18.7 us -> 23.2 us
  starting transfers between devices: 38.3 us -> 36.7 us
    unnamed x37 -> x19, local copies, waits for them, and re-layouts: 9.42 us -> 4.76 us
    pallas_call x4 -> x9, Pallas kernels: 11 us -> 14.5 us  [the longest x2 4.58 us: local(): fwd_out(flags, far, near, xb, mid, mid_acts, state, up1, bias, dn1)]
    broadcast_in_dim x5 -> x0, local copies, waits for them, and re-layouts: 1.95 us -> none  [the longest x2 1.74 us: local(): return state[:, :c].transpose(1, 0, 2)[None]]
    pad x11 -> x0, local copies, waits for them, and re-layouts: 1.81 us -> none  [the longest x7 1.06 us: by_rows(): return jnp.pad(x, ((0, 0), (0, CF - x.shape[1]), (0, 0)))]
    ppermute x12, starting transfers between devices: 38.3 us -> 36.7 us  [the longest x4 23.2 us: exchange(): far = lax.ppermute(far, 'lat', far_pairs)]
    ppermute x1 -> x0, local copies, waits for them, and re-layouts: 1.51 us -> none  [local(): nxt = by_rows(lax.ppermute(guess.astype(BF16), 'tm', back))]
    reshape x4 -> x0, local copies, waits for them, and re-layouts: 1.38 us -> none  [the longest x2 1.21 us: stack_in(): return w.transpose(1, 0, 2).reshape(w.shape[1], 9 * CB)]
    convert_element_type x1 -> x0, local copies, waits for them, and re-layouts: 0.98 us -> none  [local(): xb = by_rows(guess.astype(BF16))]
  transfers between devices with their start and end apart: 12 -> 12, of which waited for: 3 -> 5; matrix products, arithmetic and copies ran while one was open for 10% -> 1% of each run, Pallas kernels for 8% -> 19%
where the time goes in v1:
time: 86.7 us; the launch traced here: 85.4 us
  starting transfers between devices  36.7 us (42%)
  Pallas kernels  23.2 us (27%)
  waiting for transfers between devices  20.4 us (24%)
  local copies, waits for them, and re-layouts  4.86 us (6%)
    ppermute x4, starting transfers between devices, exchange(): far = lax.ppermute(far, 'lat', far_pairs)  23.2 us
    ppermute x4, waiting for transfers between devices, exchange(): far = lax.ppermute(far, 'lat', far_pairs)  19.9 us
    ppermute x4, starting transfers between devices, shift(): return lax.ppermute(x, 'tm', pairs)  11.7 us
    pallas_call x2, Pallas kernels, local(): mid, mid_acts, slope_in = fwd_in(xb, state, up1, bias, dn1)  5.11 us
    unnamed x19, local copies, waits for them, and re-layouts  4.76 us
    pallas_call x2, Pallas kernels, local(): fwd_out(flags, far, near, xb, mid, mid_acts, state, up1, bias, dn1)  4.58 us
    pallas_call x2, Pallas kernels, local(): mid, mid_rows = adj_in(lb, slope_in, up2, dn2)  3.57 us
    pallas_call x1, Pallas kernels, local(): analysis, = adj_end(*tail)  3.25 us
  transfers between devices with their start and end apart: 12, of which 5 were waited for; matrix products, arithmetic and copies ran while one was open for 1% of the time, Pallas kernels for 19%

profile of v1, /device:TPU:95, one launch (start us, length us, event | category | flops | bytes accessed | tf_op | source)
XLA Modules:
  0.0 85.4 jit_solution(12717947672010581799)
XLA Ops:
  0.1 1.3 %copy-done = f32[1,69,8,512]{3,2,1,0:T(8,128)S(1)} copy-done((f32[1,69,8,512]{3,2,1,0:T(8,128)S(1)}, f32[1,69,8,512]{3,2,1,0:T(8,128)}, u32[]{:S(2)}) %copy-start) | copy-done | bytes 1130520
  2.7 1.7 %shard_map.82 = (f32[8,72,512]{2,1,0:T(8,128)S(1)}, bf16[8,72,512]{2,1,0:T(8,128)(2,1)}, bf16[2,72,512]{2,1,0:T(8,128)(2,1)}, bf16[2,72,512]{2,1,0:T(8,128)(2,1)...) custom-call(f32[5]{0:T(128)S(1)} %convert_element_type.3.flags, f32[69,8,512]{2,1,0:T(8,128)S(1)} %bitcast.10, ...), custom_call_target="tpu_custom_call" | custom-call | bytes 4194304 | tf_op jit(solution)/shard_map/pallas_call | solution.py:307
  5.0 6.7 %collective-permute-start = (bf16[2,72,512]{2,1,0:T(8,128)(2,1)}, bf16[2,72,512]{2,1,0:T(8,128)(2,1)}, u32[]{:S(2)}, u32[]{:S(2)}) collective-permute-start(bf16[2,72,512]{2,1,0:T(8,128)(2,1)} %get-tuple-element.51), channel_id=1, source_target_pairs={{1,2},{2,1},{3,4},{4,3},{5,6},{6,5},{9,10},{10,9},{11,12},{12,11},... | collective-permute-start | bytes 442376 | tf_op jit(solution)/shard_map/ppermute | solution.py:269
  11.8 2.9 %collective-permute-start.2 = (bf16[8,72,512]{2,1,0:T(8,128)(2,1)}, bf16[8,72,512]{2,1,0:T(8,128)(2,1)S(1)}, u32[]{:S(2)}, u32[]{:S(2)}) collective-permute-start(bf16[8,72,512]{2,1,0:T(8,128)(2,1)} %get-tuple-element.45.own), channel_id=1, source_target_pairs={{8,0},{16,8},{24,16},{32,24},{40,32},{48,40},{56,48},{64,56},{72,6... | collective-permute-start | bytes 1769480 | tf_op jit(solution)/shard_map/ppermute | solution.py:274
  14.7 1.2 %copy.9.w_in = bf16[9,128,69]{2,1,0:T(8,128)(2,1)S(1)} copy(bf16[9,128,69]{1,2,0:T(8,128)(2,1)} %param.13) | data formatting | bytes 317952 | tf_op args[5]
  16.7 3.1 %shard_map.84 = (f32[4,72,512]{2,1,0:T(8,128)S(1)}, bf16[4,128,512]{2,1,0:T(8,128)(2,1)S(1)}, bf16[6,128,512]{2,1,0:T(8,128)(2,1)S(1)}) custom-call(bf16[8,72,512]{2,1,0:T(8,128)(2,1)} %get-tuple-element.45.own, f32[8,72,512]{2,1,0:T(8,128)S(1)} %get-tuple-element.46.state, bf16[128,720]{1,0:T(8,128)(2,1)S(1)} %get-tuple-element.47.wup, ...), custom_call_target="tpu_custom_call" | custom-call | flops 813957120 | bytes 4194304 | tf_op jit(solution)/shard_map/pallas_call | solution.py:313
  19.8 1.5 %collective-permute-done.far = bf16[2,72,512]{2,1,0:T(8,128)(2,1)} collective-permute-done((bf16[2,72,512]{2,1,0:T(8,128)(2,1)}, bf16[2,72,512]{2,1,0:T(8,128)(2,1)}, u32[]{:S(2)}, u32[]{:S(2)}) %collective-permute-start) | collective-permute-done | bytes 147488 | tf_op jit(solution)/shard_map/ppermute | solution.py:269
  21.3 2.6 %shard_map.85 = (bf16[8,72,512]{2,1,0:T(8,128)(2,1)S(1)}, f32[4,72,512]{2,1,0:T(8,128)S(1)}, bf16[4,128,512]{2,1,0:T(8,128)(2,1)S(1)}) custom-call(f32[5]{0:T(128)S(1)} %convert_element_type.3.flags, bf16[2,72,512]{2,1,0:T(8,128)(2,1)} %collective-permute-done.far, bf16[2,72,512]{2,1,0:T(8,128)(2,1)} %collective-permute-done.1.near, ...), custom_call_target="tpu_custom_call" | custom-call | flops 651165696 | bytes 4194304 | tf_op jit(solution)/shard_map/pallas_call | solution.py:314
  23.9 3.3 %collective-permute-start.5 = (bf16[8,72,512]{2,1,0:T(8,128)(2,1)S(1)}, bf16[8,72,512]{2,1,0:T(8,128)(2,1)S(1)}, u32[]{:S(2)}, u32[]{:S(2)}) collective-permute-start(bf16[8,72,512]{2,1,0:T(8,128)(2,1)S(1)} %get-tuple-element.67), channel_id=1, source_target_pairs={{0,8},{8,16},{16,24},{24,32},{32,40},{40,48},{48,56},{56,64},{64,7... | collective-permute-start | bytes 1769480 | tf_op jit(solution)/shard_map/ppermute | solution.py:274
  28.3 5.3 %collective-permute-start.3 = (bf16[2,72,512]{2,1,0:T(8,128)(2,1)S(1)}, bf16[2,72,512]{2,1,0:T(8,128)(2,1)S(1)}, u32[]{:S(2)}, u32[]{:S(2)}) collective-permute-start(bf16[2,72,512]{2,1,0:T(8,128)(2,1)S(1)} %get-tuple-element.57), channel_id=1, source_target_pairs={{1,2},{2,1},{3,4},{4,3},{5,6},{6,5},{9,10},{10,9},{11,12},{12,11},... | collective-permute-start | bytes 442376 | tf_op jit(solution)/shard_map/ppermute | solution.py:269
  34.1 1.8 %shard_map.88 = (f32[4,72,512]{2,1,0:T(8,128)S(1)}, bf16[4,128,512]{2,1,0:T(8,128)(2,1)S(1)}) custom-call(bf16[8,72,512]{2,1,0:T(8,128)(2,1)S(1)} %get-tuple-element.59.own, bf16[6,128,512]{2,1,0:T(8,128)(2,1)S(1)} %get-tuple-element.60.slope, bf16[128,720]{1,0:T(8,128)(2,1)S(1)} %get-tuple-element.61.wup, bf16[216,384]{1,0:T(8,128)(2,1)S(1)} %get-tuple-element.62.wdn), custom_call_target="tpu_custom_call" | custom-call | flops 813957120 | bytes 4194304 | tf_op jit(solution)/shard_map/pallas_call | solution.py:320
  35.9 8.3 %collective-permute-done.3.far = bf16[2,72,512]{2,1,0:T(8,128)(2,1)S(1)} collective-permute-done((bf16[2,72,512]{2,1,0:T(8,128)(2,1)S(1)}, bf16[2,72,512]{2,1,0:T(8,128)(2,1)S(1)}, u32[]{:S(2)}, u32[]{:S(2)}) %collective-permute-start.3) | collective-permute-done | bytes 147488 | tf_op jit(solution)/shard_map/ppermute | solution.py:269
  44.2 2.1 %shard_map.89 = (f32[8,72,512]{2,1,0:T(8,128)S(1)}, bf16[8,72,512]{2,1,0:T(8,128)(2,1)S(1)}, bf16[2,72,512]{2,1,0:T(8,128)(2,1)S(1)}, bf16[2,72,512]{2,1,0:T(8,128)(2,1)S(1)}) custom-call(f32[5]{0:T(128)S(1)} %convert_element_type.3.flags, bf16[2,72,512]{2,1,0:T(8,128)(2,1)S(1)} %collective-permute-done.3.far, ...), custom_call_target="tpu_custom_call" | custom-call | flops 651165696 | bytes 4194304 | tf_op jit(solution)/shard_map/pallas_call | solution.py:323
  46.3 5.5 %collective-permute-start.6 = (bf16[2,72,512]{2,1,0:T(8,128)(2,1)S(1)}, bf16[2,72,512]{2,1,0:T(8,128)(2,1)S(1)}, u32[]{:S(2)}, u32[]{:S(2)}) collective-permute-start(bf16[2,72,512]{2,1,0:T(8,128)(2,1)S(1)} %get-tuple-element.72), channel_id=1, source_target_pairs={{1,2},{2,1},{3,4},{4,3},{5,6},{6,5},{9,10},{10,9},{11,12},{12,11},... | collective-permute-start | bytes 442376 | tf_op jit(solution)/shard_map/ppermute | solution.py:269
  51.9 3.6 %collective-permute-start.8 = (bf16[8,72,512]{2,1,0:T(8,128)(2,1)S(1)}, bf16[8,72,512]{2,1,0:T(8,128)(2,1)S(1)}, u32[]{:S(2)}, u32[]{:S(2)}) collective-permute-start(bf16[8,72,512]{2,1,0:T(8,128)(2,1)S(1)} %get-tuple-element.69.own), channel_id=1, source_target_pairs={{8,0},{16,8},{24,16},{32,24},{40,32},{48,40},{56,48},{64,56},{72,6... | collective-permute-start | bytes 1769480 | tf_op jit(solution)/shard_map/ppermute | solution.py:274
  55.5 2.0 %shard_map.90 = (f32[4,72,512]{2,1,0:T(8,128)S(1)}, bf16[4,128,512]{2,1,0:T(8,128)(2,1)S(1)}, bf16[6,128,512]{2,1,0:T(8,128)(2,1)S(1)}) custom-call(bf16[8,72,512]{2,1,0:T(8,128)(2,1)S(1)} %get-tuple-element.69.own, f32[8,72,512]{2,1,0:T(8,128)S(1)} %get-tuple-element.70.state, bf16[128,720]{1,0:T(8,128)(2,1)S(1)} %get-tuple-element.47.wup, ...), custom_call_target="tpu_custom_call" | custom-call | flops 813957120 | bytes 4194304 | tf_op jit(solution)/shard_map/pallas_call | solution.py:313
  57.5 3.3 %collective-permute-done.6.far = bf16[2,72,512]{2,1,0:T(8,128)(2,1)S(1)} collective-permute-done((bf16[2,72,512]{2,1,0:T(8,128)(2,1)S(1)}, bf16[2,72,512]{2,1,0:T(8,128)(2,1)S(1)}, u32[]{:S(2)}, u32[]{:S(2)}) %collective-permute-start.6) | collective-permute-done | bytes 147488 | tf_op jit(solution)/shard_map/ppermute | solution.py:269
  60.8 1.9 %shard_map.91 = (bf16[8,72,512]{2,1,0:T(8,128)(2,1)S(1)}, f32[4,72,512]{2,1,0:T(8,128)S(1)}, bf16[4,128,512]{2,1,0:T(8,128)(2,1)S(1)}) custom-call(f32[5]{0:T(128)S(1)} %convert_element_type.3.flags, bf16[2,72,512]{2,1,0:T(8,128)(2,1)S(1)} %collective-permute-done.6.far, bf16[2,72,512]{2,1,0:T(8,128)(2,1)S(1)} %collective-permute-done.7.near, ...), custom_call_target="tpu_custom_call" | custom-call | flops 651165696 | bytes 4194304 | tf_op jit(solution)/shard_map/pallas_call | solution.py:314
  62.8 1.9 %collective-permute-start.11 = (bf16[8,72,512]{2,1,0:T(8,128)(2,1)S(1)}, bf16[8,72,512]{2,1,0:T(8,128)(2,1)S(1)}, u32[]{:S(2)}, u32[]{:S(2)}) collective-permute-start(bf16[8,72,512]{2,1,0:T(8,128)(2,1)S(1)} %get-tuple-element.84), channel_id=1, source_target_pairs={{0,8},{8,16},{16,24},{24,32},{32,40},{40,48},{48,56},{56,64},{64,7... | collective-permute-start | bytes 1769480 | tf_op jit(solution)/shard_map/ppermute | solution.py:274
  66.3 1.5 %collective-permute-start.10 = (bf16[2,72,512]{2,1,0:T(8,128)(2,1)S(1)}, bf16[2,72,512]{2,1,0:T(8,128)(2,1)S(1)}, u32[]{:S(2)}, u32[]{:S(2)}) collective-permute-start(bf16[2,72,512]{2,1,0:T(8,128)(2,1)S(1)} %get-tuple-element.77), channel_id=1, source_target_pairs={{0,1},{1,0},{2,3},{3,2},{4,5},{5,4},{6,7},{7,6},{8,9},{9,8},{10,11... | collective-permute-start | bytes 442376 | tf_op jit(solution)/shard_map/ppermute | solution.py:270
  67.8 5.8 %collective-permute-start.9 = (bf16[2,72,512]{2,1,0:T(8,128)(2,1)S(1)}, bf16[2,72,512]{2,1,0:T(8,128)(2,1)S(1)}, u32[]{:S(2)}, u32[]{:S(2)}) collective-permute-start(bf16[2,72,512]{2,1,0:T(8,128)(2,1)S(1)} %get-tuple-element.76), channel_id=1, source_target_pairs={{1,2},{2,1},{3,4},{4,3},{5,6},{6,5},{9,10},{10,9},{11,12},{12,11},... | collective-permute-start | bytes 442376 | tf_op jit(solution)/shard_map/ppermute | solution.py:269
  73.6 1.8 %shard_map.93 = (f32[4,72,512]{2,1,0:T(8,128)S(1)}, bf16[4,128,512]{2,1,0:T(8,128)(2,1)S(1)}) custom-call(bf16[8,72,512]{2,1,0:T(8,128)(2,1)S(1)} %get-tuple-element.78.own, bf16[6,128,512]{2,1,0:T(8,128)(2,1)S(1)} %get-tuple-element.79.slope, bf16[128,720]{1,0:T(8,128)(2,1)S(1)} %get-tuple-element.61.wup, bf16[216,384]{1,0:T(8,128)(2,1)S(1)} %get-tuple-element.62.wdn), custom_call_target="tpu_custom_call" | custom-call | flops 813957120 | bytes 4194304 | tf_op jit(solution)/shard_map/pallas_call | solution.py:320
  75.4 6.7 %collective-permute-done.9.far = bf16[2,72,512]{2,1,0:T(8,128)(2,1)S(1)} collective-permute-done((bf16[2,72,512]{2,1,0:T(8,128)(2,1)S(1)}, bf16[2,72,512]{2,1,0:T(8,128)(2,1)S(1)}, u32[]{:S(2)}, u32[]{:S(2)}) %collective-permute-start.9) | collective-permute-done | bytes 147488 | tf_op jit(solution)/shard_map/ppermute | solution.py:269
  82.1 3.3 %shard_map.94 = f32[69,8,512]{2,1,0:T(8,128)} custom-call(f32[5]{0:T(128)S(1)} %convert_element_type.3.flags, bf16[2,72,512]{2,1,0:T(8,128)(2,1)S(1)} %collective-permute-done.9.far, bf16[2,72,512]{2,1,0:T(8,128)(2,1)S(1)} %collective-permute-done.10.near, bf16[8,72,512]{2,1,0:T(8,128)(2,1)S(1)} %get-tuple-element.78.own, ...), custom_call_target="tpu_custom_call" | custom-call | flops 651165696 | bytes 4194304 | tf_op jit(solution)/shard_map/pallas_call | solution.py:325
  (34 shorter events, 6.2 us)
Async XLA Ops:
  0.1 1.3 %copy-start = (f32[1,69,8,512]{3,2,1,0:T(8,128)S(1)}, f32[1,69,8,512]{3,2,1,0:T(8,128)}, u32[]{:S(2)}) copy-start(f32[1,69,8,512]{3,2,1,0:T(8,128)} %param.8) | copy-start | bytes 3391492
  1.4 0.7 copy-start.7
  2.0 0.7 copy-start.8
  2.7 13.2 %copy-start.1 = (f32[1,69,8,512]{3,2,1,0:T(8,128)S(1)}, f32[1,69,8,512]{3,2,1,0:T(8,128)}, u32[]{:S(2)}) copy-start(f32[1,69,8,512]{3,2,1,0:T(8,128)} %param.10) | copy-start | bytes 3391492
  2.7 13.2 %copy-start.3 = (bf16[9,69,128]{2,1,0:T(8,128)(2,1)S(1)}, bf16[9,69,128]{2,1,0:T(8,128)(2,1)}, u32[]{:S(2)}) copy-start(bf16[9,69,128]{2,1,0:T(8,128)(2,1)} %w_out.3) | copy-start | bytes 476932
  4.4 0.6 copy-start.4
  5.0 16.2 %collective-permute-start = (bf16[2,72,512]{2,1,0:T(8,128)(2,1)}, bf16[2,72,512]{2,1,0:T(8,128)(2,1)}, u32[]{:S(2)}, u32[]{:S(2)}) collective-permute-start(bf16[2,72,512]{2,1,0:T(8,128)(2,1)} %get-tuple-element.51), channel_id=1, source_target_pairs={{1,2},{2,1},{3,4},{4,3},{5,6},{6,5},{9,10},{10,9},{11,12},{12,11},... | collective-permute-start | bytes 442376 | tf_op jit(solution)/shard_map/ppermute | solution.py:269
  11.7 9.6 %collective-permute-start.1 = (bf16[2,72,512]{2,1,0:T(8,128)(2,1)}, bf16[2,72,512]{2,1,0:T(8,128)(2,1)}, u32[]{:S(2)}, u32[]{:S(2)}) collective-permute-start(bf16[2,72,512]{2,1,0:T(8,128)(2,1)} %get-tuple-element.52), channel_id=1, source_target_pairs={{0,1},{1,0},{2,3},{3,2},{4,5},{5,4},{6,7},{7,6},{8,9},{9,8},{10,11... | collective-permute-start | bytes 442376 | tf_op jit(solution)/shard_map/ppermute | solution.py:270
  11.8 15.5 %collective-permute-start.2 = (bf16[8,72,512]{2,1,0:T(8,128)(2,1)}, bf16[8,72,512]{2,1,0:T(8,128)(2,1)S(1)}, u32[]{:S(2)}, u32[]{:S(2)}) collective-permute-start(bf16[8,72,512]{2,1,0:T(8,128)(2,1)} %get-tuple-element.45.own), channel_id=1, source_target_pairs={{8,0},{16,8},{24,16},{32,24},{40,32},{48,40},{56,48},{64,56},{72,6... | collective-permute-start | bytes 1769480 | tf_op jit(solution)/shard_map/ppermute | solution.py:274
  15.8 0.9 copy-start.5
  21.3 6.0 %copy-start.6 = (s32[1,8,512]{2,1,0:T(8,128)S(1)}, s32[1,8,512]{2,1,0:T(8,128)}, u32[]{:S(2)}) copy-start(s32[1,8,512]{2,1,0:T(8,128)} %param.11) | copy-start | bytes 49156
  23.9 20.3 %collective-permute-start.5 = (bf16[8,72,512]{2,1,0:T(8,128)(2,1)S(1)}, bf16[8,72,512]{2,1,0:T(8,128)(2,1)S(1)}, u32[]{:S(2)}, u32[]{:S(2)}) collective-permute-start(bf16[8,72,512]{2,1,0:T(8,128)(2,1)S(1)} %get-tuple-element.67), channel_id=1, source_target_pairs={{0,8},{8,16},{16,24},{24,32},{32,40},{40,48},{48,56},{56,64},{64,7... | collective-permute-start | bytes 1769480 | tf_op jit(solution)/shard_map/ppermute | solution.py:274
  27.3 6.4 %copy-start.2 = (f32[69,8,512]{2,1,0:T(8,128)S(1)}, f32[69,8,512]{2,1,0:T(8,128)}, u32[]{:S(2)}) copy-start(f32[69,8,512]{2,1,0:T(8,128)} %field.1) | copy-start | bytes 3391492
  28.3 15.9 %collective-permute-start.3 = (bf16[2,72,512]{2,1,0:T(8,128)(2,1)S(1)}, bf16[2,72,512]{2,1,0:T(8,128)(2,1)S(1)}, u32[]{:S(2)}, u32[]{:S(2)}) collective-permute-start(bf16[2,72,512]{2,1,0:T(8,128)(2,1)S(1)} %get-tuple-element.57), channel_id=1, source_target_pairs={{1,2},{2,1},{3,4},{4,3},{5,6},{6,5},{9,10},{10,9},{11,12},{12,11},... | collective-permute-start | bytes 442376 | tf_op jit(solution)/shard_map/ppermute | solution.py:269
  33.6 10.6 %collective-permute-start.4 = (bf16[2,72,512]{2,1,0:T(8,128)(2,1)S(1)}, bf16[2,72,512]{2,1,0:T(8,128)(2,1)S(1)}, u32[]{:S(2)}, u32[]{:S(2)}) collective-permute-start(bf16[2,72,512]{2,1,0:T(8,128)(2,1)S(1)} %get-tuple-element.58), channel_id=1, source_target_pairs={{0,1},{1,0},{2,3},{3,2},{4,5},{5,4},{6,7},{7,6},{8,9},{9,8},{10,11... | collective-permute-start | bytes 442376 | tf_op jit(solution)/shard_map/ppermute | solution.py:270
  46.3 14.5 %collective-permute-start.6 = (bf16[2,72,512]{2,1,0:T(8,128)(2,1)S(1)}, bf16[2,72,512]{2,1,0:T(8,128)(2,1)S(1)}, u32[]{:S(2)}, u32[]{:S(2)}) collective-permute-start(bf16[2,72,512]{2,1,0:T(8,128)(2,1)S(1)} %get-tuple-element.72), channel_id=1, source_target_pairs={{1,2},{2,1},{3,4},{4,3},{5,6},{6,5},{9,10},{10,9},{11,12},{12,11},... | collective-permute-start | bytes 442376 | tf_op jit(solution)/shard_map/ppermute | solution.py:269
  51.8 9.0 %collective-permute-start.7 = (bf16[2,72,512]{2,1,0:T(8,128)(2,1)S(1)}, bf16[2,72,512]{2,1,0:T(8,128)(2,1)S(1)}, u32[]{:S(2)}, u32[]{:S(2)}) collective-permute-start(bf16[2,72,512]{2,1,0:T(8,128)(2,1)S(1)} %get-tuple-element.73), channel_id=1, source_target_pairs={{0,1},{1,0},{2,3},{3,2},{4,5},{5,4},{6,7},{7,6},{8,9},{9,8},{10,11... | collective-permute-start | bytes 442376 | tf_op jit(solution)/shard_map/ppermute | solution.py:270
  51.9 13.3 %collective-permute-start.8 = (bf16[8,72,512]{2,1,0:T(8,128)(2,1)S(1)}, bf16[8,72,512]{2,1,0:T(8,128)(2,1)S(1)}, u32[]{:S(2)}, u32[]{:S(2)}) collective-permute-start(bf16[8,72,512]{2,1,0:T(8,128)(2,1)S(1)} %get-tuple-element.69.own), channel_id=1, source_target_pairs={{8,0},{16,8},{24,16},{32,24},{40,32},{48,40},{56,48},{64,56},{72,6... | collective-permute-start | bytes 1769480 | tf_op jit(solution)/shard_map/ppermute | solution.py:274
  62.8 19.4 %collective-permute-start.11 = (bf16[8,72,512]{2,1,0:T(8,128)(2,1)S(1)}, bf16[8,72,512]{2,1,0:T(8,128)(2,1)S(1)}, u32[]{:S(2)}, u32[]{:S(2)}) collective-permute-start(bf16[8,72,512]{2,1,0:T(8,128)(2,1)S(1)} %get-tuple-element.84), channel_id=1, source_target_pairs={{0,8},{8,16},{16,24},{24,32},{32,40},{40,48},{48,56},{56,64},{64,7... | collective-permute-start | bytes 1769480 | tf_op jit(solution)/shard_map/ppermute | solution.py:274
  66.3 9.1 %collective-permute-start.10 = (bf16[2,72,512]{2,1,0:T(8,128)(2,1)S(1)}, bf16[2,72,512]{2,1,0:T(8,128)(2,1)S(1)}, u32[]{:S(2)}, u32[]{:S(2)}) collective-permute-start(bf16[2,72,512]{2,1,0:T(8,128)(2,1)S(1)} %get-tuple-element.77), channel_id=1, source_target_pairs={{0,1},{1,0},{2,3},{3,2},{4,5},{5,4},{6,7},{7,6},{8,9},{9,8},{10,11... | collective-permute-start | bytes 442376 | tf_op jit(solution)/shard_map/ppermute | solution.py:270
  67.8 14.3 %collective-permute-start.9 = (bf16[2,72,512]{2,1,0:T(8,128)(2,1)S(1)}, bf16[2,72,512]{2,1,0:T(8,128)(2,1)S(1)}, u32[]{:S(2)}, u32[]{:S(2)}) collective-permute-start(bf16[2,72,512]{2,1,0:T(8,128)(2,1)S(1)} %get-tuple-element.76), channel_id=1, source_target_pairs={{1,2},{2,1},{3,4},{4,3},{5,6},{6,5},{9,10},{10,9},{11,12},{12,11},... | collective-permute-start | bytes 442376 | tf_op jit(solution)/shard_map/ppermute | solution.py:269

commit v2 on v1

v2 whole, which is shorter than its diff:
```python
import functools

import jax
import jax.numpy as jnp
from jax import lax
from jax.experimental import pallas as pl
from jax.experimental.pallas import tpu as pltpu
from jax.sharding import PartitionSpec as P


ITERS = 2
STEP = 0.25
CF = 72
CB = 80
VMEM = pl.BlockSpec(memory_space=pltpu.VMEM)
SMEM = pl.BlockSpec(memory_space=pltpu.SMEM)
F32, BF16 = jnp.float32, jnp.bfloat16


def dot(a, b):
    return jnp.dot(a, b, preferred_element_type=F32)


def shifted_sum(y):
    lon = y.shape[1]
    left = pltpu.roll(y[:CF], 1, 1)
    right = pltpu.roll(y[2 * CF :], lon - 1, 1)
    return y[CF : 2 * CF] + left + right


def place_row(dst, j, row):
    x = row.astype(F32)
    lon = x.shape[1]
    pad = jnp.zeros((CB - x.shape[0], lon), F32)
    for i, v in enumerate((pltpu.roll(x, 1, 1), x, pltpu.roll(x, lon - 1, 1))):
        dst[pl.ds((3 * j + i) * CB, CB), :] = jnp.concatenate([v, pad], axis=0).astype(BF16)


def window(ref, j, unit):
    return ref[pl.ds(j * unit, 3 * unit), :]


def own_row(edge, inner, r):
    n = edge.shape[0] + inner.shape[0]
    return edge[r] if r < 2 else inner[r - 2] if r < n - 2 else edge[r - n + 4]


def edge_rows(n):
    return 0, 1, n - 2, n - 1


def halos(flags, far, near, i):
    odd = flags[4] > 0.5
    a, b = far[i].astype(F32), near[i].astype(F32)
    return jnp.where(odd, b, a), jnp.where(odd, a, b)


def send_edges(flags, rows, far_out, near_out):
    odd = flags[4] > 0.5
    for i in range(2):
        low, high = rows[i], rows[2 + i]
        far_out[i] = jnp.where(odd, high, low).astype(BF16)
        near_out[i] = jnp.where(odd, low, high).astype(BF16)


def column(row, size):
    m = row.shape[1]
    at = lax.broadcasted_iota(jnp.int32, (size, m), 0) == lax.broadcasted_iota(jnp.int32, (size, m), 1)
    return jnp.sum(jnp.where(at, row, 0.0), axis=1, keepdims=True)


def padded(v, size):
    return jnp.concatenate([v, jnp.zeros((size - v.shape[0], v.shape[1]), F32)], axis=0)


def stack_in(taps, out):
    width = out.shape[1]
    whole = padded(jnp.concatenate([padded(t, CB) for t in taps], axis=0), -(-width // 128) * 128)
    for at in range(0, width, 128):
        size = min(128, width - at)
        out[:, at : at + size] = whole[at : at + 128].T[:, :size].astype(BF16)


def stack_out(taps, out):
    hid = taps[0].shape[1]
    for dr in range(3):
        rows = jnp.concatenate([padded(t, CF) for t in taps[3 * dr : 3 * dr + 3]], axis=0)
        out[:, dr * hid : (dr + 1) * hid] = rows.astype(BF16)


def prepare(flags, guess, state_e, state_i, xb_out, far_out, near_out):
    n = guess.shape[1]
    rows = [padded(guess[:, r, :], CF) for r in edge_rows(n)]
    send_edges(flags, rows, far_out, near_out)
    for i, row in enumerate(rows):
        state_e[i] = row
        xb_out[i] = row.astype(BF16)
    for i in range(n - 4):
        row = padded(guess[:, i + 2, :], CF)
        state_i[i] = row
        xb_out[4 + i] = row.astype(BF16)


def prepare_forward(w_in, w_out, field, b_row, chan_row, up_out, down_out, rows_out, bias_out, chan_out):
    stack_in([w_in[t].astype(F32) for t in range(9)], up_out)
    stack_out([w_out[t].astype(F32) for t in range(9)], down_out)
    for r in range(field.shape[1]):
        rows_out[r] = padded(field[:, r, :], CF)
    bias_out[...] = jnp.broadcast_to(column(b_row[...], bias_out.shape[0]), bias_out.shape)
    chan_out[...] = jnp.broadcast_to(column(chan_row[...].astype(F32), CF), chan_out.shape)


def prepare_adjoint(w_in, w_out, field, up_out, down_out, rows_out):
    stack_in([w_out[8 - t].astype(F32) for t in range(9)], up_out)
    stack_out([w_in[8 - t].astype(F32) for t in range(9)], down_out)
    for r in range(field.shape[1]):
        rows_out[r] = padded(field[:, r, :], CF)


def wide(bias, lon):
    return jnp.concatenate([bias[...]] * (lon // bias.shape[1]), axis=1)


def activate(wup, bias, xs, at):
    z = dot(wup[...], window(xs, at, 3 * CB)) + wide(bias, xs.shape[1])
    s = jax.nn.sigmoid(z)
    act = z * s
    return act, s + act * (1.0 - s)


def inner_forward(joined, own_e, own_i, state, wup, bias, wdn, fore_out, send_out, acts_out, slope_out, xs, acts):
    if joined:
        own_e, own_i = own_e.at[:4], own_e.at[4:]
    n, hid = own_e.shape[0] + own_i.shape[0], bias.shape[0]

    def up(j):
        act, slope = activate(wup, bias, xs, j - 1)
        slope_out[j - 1] = slope.astype(BF16)
        act = act.astype(BF16)
        acts[pl.ds((j - 1) * hid, hid), :] = act
        if j in (1, 2):
            acts_out[j - 1] = act
        if j in (n - 3, n - 2):
            acts_out[j - n + 5] = act

    def down(i):
        fore = state[i] + shifted_sum(dot(wdn[...], window(acts, i, hid)))
        fore_out[i] = fore
        send_out[i] = fore.astype(BF16)

    for j in range(2):
        place_row(xs, j, own_row(own_e, own_i, j))
    for j in range(1, n - 1):
        place_row(xs, j + 1, own_row(own_e, own_i, j + 1))
        up(j)
        if j >= 3:
            down(j - 3)


def misfit(has_next, st, fore, obs, nxt, cell, chan):
    lam = chan[...] * cell.astype(F32) * (fore - obs) - has_next * (nxt.astype(F32) - fore)
    return lam, st - STEP * (st + lam)


def inner_misfit(flags, fore, state, obs, nxt, cell, chan, lb_out, acc_out):
    skip = nxt.shape[0] - state.shape[0]
    for i in range(state.shape[0]):
        lam, acc = misfit(flags[2], state[i], fore[i], obs[i + 2], nxt[i + skip], cell[pl.ds(i + 2, 1), :], chan)
        lb_out[i] = lam.astype(BF16)
        acc_out[i] = acc


def place_edges(flags, far, near, own, inner, xs, hidden, hid):
    for i in range(2):
        below, above = halos(flags, far, near, i)
        place_row(xs, i, below)
        place_row(xs, 2 + i, own[i])
        place_row(xs, 4 + i, own[2 + i])
        place_row(xs, 6 + i, above)
        hidden[pl.ds((2 + i) * hid, hid), :] = inner[i]
        hidden[pl.ds((4 + i) * hid, hid), :] = inner[2 + i]


def edge_forward(flags, far, near, own, inner_acts, state, obs, nxt, cell, chan, wup, bias, wdn,
                 send_out, lb_out, far_out, near_out, slope_out, acc_out, xs, acts):
    n, hid = obs.shape[0], bias.shape[0]
    place_edges(flags, far, near, own, inner_acts, xs, acts, hid)
    for i, (x_at, act_at, inside) in enumerate(
        ((0, 0, flags[0]), (1, 1, None), (4, 6, None), (5, 7, flags[1]))
    ):
        act, slope = activate(wup, bias, xs, x_at)
        if inside is not None:
            act, slope = act * inside, slope * inside
        acts[pl.ds(act_at * hid, hid), :] = act.astype(BF16)
        slope_out[i] = slope.astype(BF16)
    lams = []
    for i, (r, at) in enumerate(zip(edge_rows(n), (0, 1, 4, 5))):
        fore = state[i] + shifted_sum(dot(wdn[...], window(acts, at, hid)))
        send_out[i] = fore.astype(BF16)
        lam, acc = misfit(flags[2], state[i], fore, obs[r], nxt[i], cell[pl.ds(r, 1), :], chan)
        lb_out[i] = lam.astype(BF16)
        acc_out[i] = acc
        lams.append(lam)
    send_edges(flags, lams, far_out, near_out)


def descend(flags, acc, prev, ground, grad):
    earlier = jnp.where(flags[3] > 0.5, ground, prev.astype(F32))
    return acc + STEP * (earlier - grad)


def inner_adjoint(flags, own_e, own_i, slope, acc, prev, ground, wup, wdn, state_out, xb_out, rows_out, xs, grads):
    n, hid = own_e.shape[0] + own_i.shape[0], slope.shape[1]

    def up(j):
        g = (dot(wup[...], window(xs, j - 1, 3 * CB)) * slope[j - 1].astype(F32)).astype(BF16)
        grads[pl.ds((j - 1) * hid, hid), :] = g
        if j in (1, 2):
            rows_out[j - 1] = g
        if j in (n - 3, n - 2):
            rows_out[j - n + 5] = g

    def down(i):
        grad = shifted_sum(dot(wdn[...], window(grads, i, hid)))
        st = descend(flags, acc[i], prev[i], ground[i + 2], grad)
        state_out[i] = st
        xb_out[i] = st.astype(BF16)

    for j in range(2):
        place_row(xs, j, own_row(own_e, own_i, j))
    for j in range(1, n - 1):
        place_row(xs, j + 1, own_row(own_e, own_i, j + 1))
        up(j)
        if j >= 3:
            down(j - 3)


def edge_states(flags, far, near, own, inner_rows, slope, acc, prev, ground, wup, wdn, xs, grads):
    n, hid = ground.shape[0], slope.shape[1]
    place_edges(flags, far, near, own, inner_rows, xs, grads, hid)
    for i, (x_at, at) in enumerate(((0, 0), (1, 1), (4, 6), (5, 7))):
        g = dot(wup[...], window(xs, x_at, 3 * CB)) * slope[i].astype(F32)
        grads[pl.ds(at * hid, hid), :] = g.astype(BF16)
    return [
        descend(flags, acc[i], prev[i], ground[r], shifted_sum(dot(wdn[...], window(grads, at, hid))))
        for i, (r, at) in enumerate(zip(edge_rows(n), (0, 1, 4, 5)))
    ]


def edge_adjoint(*refs):
    (state_out, xb_out, far_out, near_out), scratch = refs[11:15], refs[15:]
    rows = edge_states(*refs[:11], *scratch)
    send_edges(refs[0], rows, far_out, near_out)
    for i, row in enumerate(rows):
        state_out[i] = row
        xb_out[i] = row.astype(BF16)


def last_adjoint(*refs):
    inner, out, scratch = refs[11], refs[12], refs[13:]
    c, n = out.shape[:2]
    for r in range(2, n - 2):
        out[:, r, :] = inner[r - 2][:c]
    for r, row in zip(edge_rows(n), edge_states(*refs[:11], *scratch)):
        out[:, r, :] = row[:c]


def local(first_guess, background, observed, cell_mask, chan_mask, w_in, b_in, w_out):
    c, n, lon = first_guess.shape[1:]
    hid = b_in.shape[0]
    lat, lats = lax.axis_index("lat"), lax.axis_size("lat")
    tm, tms = lax.axis_index("tm"), lax.axis_size("tm")
    odd = lat % 2 == 1
    flags = jnp.stack([lat > 0, lat < lats - 1, tm < tms - 1, tm == 0, odd]).astype(F32)
    near_pairs = [p for i in range(0, lats - 1, 2) for p in ((i, i + 1), (i + 1, i))]
    far_pairs = [p for i in range(1, lats - 1, 2) for p in ((i, i + 1), (i + 1, i))]
    ahead = [(i, i + 1) for i in range(tms - 1)]
    back = [(j, i) for i, j in ahead]

    def exchange(far, near):
        far = lax.ppermute(far, "lat", far_pairs)
        near = lax.ppermute(near, "lat", near_pairs)
        return far, near

    def shift(x, pairs):
        return lax.ppermute(x, "tm", pairs)

    cell = cell_mask[0]
    w_in = w_in.transpose(0, 2, 1)
    S = jax.ShapeDtypeStruct
    rows = S((n, CF, lon), F32)
    edge, four_f, four_b = S((2, CF, lon), BF16), S((4, CF, lon), F32), S((4, CF, lon), BF16)
    mid_f, mid_b = S((n - 4, CF, lon), F32), S((n - 4, CF, lon), BF16)
    four_h, six_h = S((4, hid, lon), BF16), S((n - 2, hid, lon), BF16)
    ups, downs = S((hid, 9 * CB), BF16), S((3 * CF, 3 * hid), BF16)
    bias_s, chan_s = S((hid, 128), F32), S((CF, lon), F32)
    unit = 2 * 9 * c * hid * lon

    def call(body, count, outs, held=0, work=0, flagged=True):
        return pl.pallas_call(
            body,
            out_shape=outs,
            in_specs=[SMEM] * flagged + [VMEM] * count,
            out_specs=(VMEM,) * len(outs),
            scratch_shapes=[pltpu.VMEM((8 * 3 * CB, lon), BF16), pltpu.VMEM((held * hid, lon), BF16)] if held else [],
            compiler_params=pltpu.CompilerParams(vmem_limit_bytes=16 * 2**20),
            cost_estimate=pl.CostEstimate(flops=work * unit, bytes_accessed=4 * 2**20, transcendentals=0),
        )

    state_e, state_i, xb_e, far, near = call(prepare, 1, (four_f, mid_f, S((n, CF, lon), BF16), edge, edge))(
        flags, first_guess[0])
    xb_i = nxt_i = None
    for step in range(ITERS):
        joined = xb_i is None
        far, near = exchange(far, near)
        nxt_e = shift(xb_e, back)
        if joined:
            nxt_i = nxt_e
            up1, dn1, obs, bias, chan = call(
                prepare_forward, 5, (ups, downs, rows, bias_s, chan_s), work=4, flagged=False
            )(w_in, w_out, observed[0], b_in[None], chan_mask)
        fore_i, send, mid_acts, slope_i = call(
            functools.partial(inner_forward, joined), 6, (mid_f, mid_b, four_h, six_h), n - 2, 10, False,
        )(xb_e, xb_e if joined else xb_i, state_i, up1, bias, dn1)
        prev_i = shift(send, ahead)
        send, lb_e, far, near, slope_e, acc_e = call(
            edge_forward, 12, (four_b, four_b, edge, edge, four_h, four_f), 8, 8
        )(flags, far, near, xb_e, mid_acts, state_e, obs, nxt_e, cell, chan, up1, bias, dn1)
        far, near = exchange(far, near)
        prev_e = shift(send, ahead)
        lb_i, acc_i = call(inner_misfit, 6, (mid_b, mid_f))(flags, fore_i, state_i, obs, nxt_i, cell, chan)
        if step == 0:
            up2, dn2, ground = call(
                prepare_adjoint, 3, (ups, downs, rows), work=4, flagged=False
            )(w_in, w_out, background)
        state_i, xb_i, mid_rows = call(
            inner_adjoint, 8, (mid_f, mid_b, four_h), n - 2, 10
        )(flags, lb_e, lb_i, slope_i, acc_i, prev_i, ground, up2, dn2)
        tail = (flags, far, near, lb_e, mid_rows, slope_e, acc_e, prev_e, ground, up2, dn2)
        if step < ITERS - 1:
            nxt_i = shift(xb_i, back)
            state_e, xb_e, far, near = call(edge_adjoint, 10, (four_f, four_b, edge, edge), 8, 8)(*tail)
        else:
            (analysis,) = call(last_adjoint, 11, (S((c, n, lon), F32),), 8, 8)(*tail, state_i)
    return analysis[None]


def solution(mesh):
    return jax.shard_map(
        local,
        mesh=mesh,
        in_specs=(
            P("tm", None, "lat", None),
            P(None, "lat", None),
            P("tm", None, "lat", None),
            P("tm", "lat", None),
            P("tm", None),
            P(),
            P(),
            P(),
        ),
        out_specs=P("tm", None, "lat", None),
        check_vma=False,
    )
```

time: 86.7 us -> 88.6 us (1.022); the launches traced: 85.4 us -> 88.2 us
  starting transfers between devices: 36.7 us -> 51 us
  waiting for transfers between devices: 20.4 us -> 11.6 us
  local copies, waits for them, and re-layouts: 4.86 us -> 3.29 us
  Pallas kernels: 23.2 us -> 22 us
    ppermute x4 -> x7, starting transfers between devices: 11.7 us -> 24.5 us  [shift(): return lax.ppermute(x, 'tm', pairs)]
    ppermute x4, waiting for transfers between devices: 19.9 us -> 11.5 us  [exchange(): far = lax.ppermute(far, 'lat', far_pairs)]
    ppermute x4, starting transfers between devices: 23.2 us -> 26.2 us  [exchange(): far = lax.ppermute(far, 'lat', far_pairs)]
    unnamed x19 -> x20, local copies, waits for them, and re-layouts: 4.76 us -> 3.19 us
    ppermute x4, starting transfers between devices: 1.81 us -> 0.37 us  [exchange(): near = lax.ppermute(near, 'lat', near_pairs)]
    pallas_call x13, Pallas kernels: 23.2 us -> 22 us  [the longest x2 5.5 us: local(): call(inner_adjoint, 8, (mid_f, mid_b, four_h), n - 2, 10)]
  transfers between devices with their start and end apart: 12 -> 15, of which waited for: 5 -> 2; matrix products, arithmetic and copies ran while one was open for 1% -> 0% of each run, Pallas kernels for 19% -> 18%
where the time goes in v2:
time: 88.6 us; the launch traced here: 88.2 us
  starting transfers between devices  51 us (58%)
  Pallas kernels  22 us (25%)
  waiting for transfers between devices  11.6 us (13%)
  local copies, waits for them, and re-layouts  3.29 us (4%)
    ppermute x4, starting transfers between devices, exchange(): far = lax.ppermute(far, 'lat', far_pairs)  26.2 us
    ppermute x7, starting transfers between devices, shift(): return lax.ppermute(x, 'tm', pairs)  24.5 us
    ppermute x4, waiting for transfers between devices, exchange(): far = lax.ppermute(far, 'lat', far_pairs)  11.5 us
    pallas_call x2, Pallas kernels, local(): call(inner_adjoint, 8, (mid_f, mid_b, four_h), n - 2, 10)  5.5 us
    pallas_call x2, Pallas kernels, local(): call(edge_forward, 12, (four_b, four_b, edge, edge, four_h, four_f), 8, 8)  4.21 us
    pallas_call x2, Pallas kernels, local(): call(functools.partial(inner_forward, joined), 6, (mid_f, mid_b, four_h,...  4.08 us
    unnamed x20, local copies, waits for them, and re-layouts  3.19 us
    pallas_call x1, Pallas kernels, local(): call(last_adjoint, 11, (S((c, n, lon), F32),), 8, 8)(*tail, state_i)  3.12 us
  transfers between devices with their start and end apart: 15, of which 2 were waited for; matrix products, arithmetic and copies ran while one was open for 0% of the time, Pallas kernels for 18%

profile of v2, /device:TPU:95, one launch (start us, length us, event | category | flops | bytes accessed | tf_op | source)
XLA Modules:
  0.0 88.2 jit_solution(1197288066210780694)
XLA Ops:
  0.1 1.3 %copy-done.2 = f32[1,69,8,512]{3,2,1,0:T(8,128)S(1)} copy-done((f32[1,69,8,512]{3,2,1,0:T(8,128)S(1)}, f32[1,69,8,512]{3,2,1,0:T(8,128)}, u32[]{:S(2)}) %copy-start.2) | copy-done | bytes 1130520
  2.3 2.6 %collective-permute-start.2 = (bf16[8,72,512]{2,1,0:T(8,128)(2,1)S(1)}, bf16[8,72,512]{2,1,0:T(8,128)(2,1)S(1)}, u32[]{:S(2)}, u32[]{:S(2)}) collective-permute-start(bf16[8,72,512]{2,1,0:T(8,128)(2,1)S(1)} %get-tuple-element.53.own_e.own_i.own), channel_id=1, source_target_pairs={{8,0},{16,8},{24,16},{32,24},{40,32},{48,40},{56,48},{64,56},{72,6... | collective-permute-start | bytes 1769480 | tf_op jit(solution)/shard_map/ppermute | solution.py:286
  4.9 6.7 %collective-permute-start = (bf16[2,72,512]{2,1,0:T(8,128)(2,1)S(1)}, bf16[2,72,512]{2,1,0:T(8,128)(2,1)S(1)}, u32[]{:S(2)}, u32[]{:S(2)}) collective-permute-start(bf16[2,72,512]{2,1,0:T(8,128)(2,1)S(1)} %get-tuple-element.51), channel_id=1, source_target_pairs={{1,2},{2,1},{3,4},{4,3},{5,6},{6,5},{9,10},{10,9},{11,12},{12,11},... | collective-permute-start | bytes 442376 | tf_op jit(solution)/shard_map/ppermute | solution.py:281
  11.7 0.9 %copy-done.3 = bf16[9,128,69]{1,2,0:T(8,128)(2,1)S(1)} copy-done((bf16[9,128,69]{1,2,0:T(8,128)(2,1)S(1)}, bf16[9,128,69]{1,2,0:T(8,128)(2,1)}, u32[]{:S(2)}) %copy-start.3) | copy-done | bytes 159000
  12.6 0.9 %copy-done.5 = bf16[9,69,128]{2,1,0:T(8,128)(2,1)S(1)} copy-done((bf16[9,69,128]{2,1,0:T(8,128)(2,1)S(1)}, bf16[9,69,128]{2,1,0:T(8,128)(2,1)}, u32[]{:S(2)}) %copy-start.5) | copy-done | bytes 159000
  14.0 2.0 %shard_map.84 = (f32[4,72,512]{2,1,0:T(8,128)S(1)}, bf16[4,72,512]{2,1,0:T(8,128)(2,1)S(1)}, bf16[4,128,512]{2,1,0:T(8,128)(2,1)S(1)}, bf16[6,128,512]{2,1,0:T(8,128)(2,1)S(1)}) custom-call(bf16[8,72,512]{2,1,0:T(8,128)(2,1)S(1)} %get-tuple-element.53.own_e.own_i.own, bf16[8,72,512]{2,1,0:T(8,128)(2,1)S(1)} %get-tuple-element.53.own_e.own_i.own, ...), custom_call_target="tpu_custom_call" | custom-call | flops 813957120 | bytes 4194304 | tf_op jit(solution)/shard_map/pallas_call | solution.py:322
  16.0 5.4 %collective-permute-start.5 = (bf16[4,72,512]{2,1,0:T(8,128)(2,1)S(1)}, bf16[4,72,512]{2,1,0:T(8,128)(2,1)S(1)}, u32[]{:S(2)}, u32[]{:S(2)}) collective-permute-start(bf16[4,72,512]{2,1,0:T(8,128)(2,1)S(1)} %get-tuple-element.69), channel_id=1, source_target_pairs={{0,8},{8,16},{16,24},{24,32},{32,40},{40,48},{48,56},{56,64},{64,7... | collective-permute-start | bytes 884744 | tf_op jit(solution)/shard_map/ppermute | solution.py:286
  21.5 2.1 %shard_map.85 = (bf16[4,72,512]{2,1,0:T(8,128)(2,1)S(1)}, bf16[4,72,512]{2,1,0:T(8,128)(2,1)S(1)}, bf16[2,72,512]{2,1,0:T(8,128)(2,1)S(1)}, bf16[2,72,512]{2,1,0...) custom-call(f32[5]{0:T(128)S(1)} %convert_element_type.3.flags.refs_0_, ...), custom_call_target="tpu_custom_call" | custom-call | flops 651165696 | bytes 4194304 | tf_op jit(solution)/shard_map/pallas_call | solution.py:326
  23.6 4.7 %collective-permute-start.6 = (bf16[4,72,512]{2,1,0:T(8,128)(2,1)S(1)}, bf16[4,72,512]{2,1,0:T(8,128)(2,1)S(1)}, u32[]{:S(2)}, u32[]{:S(2)}) collective-permute-start(bf16[4,72,512]{2,1,0:T(8,128)(2,1)S(1)} %get-tuple-element.76), channel_id=1, source_target_pairs={{0,8},{8,16},{16,24},{24,32},{32,40},{40,48},{48,56},{56,64},{64,7... | collective-permute-start | bytes 884744 | tf_op jit(solution)/shard_map/ppermute | solution.py:286
  28.3 4.6 %collective-permute-start.3 = (bf16[2,72,512]{2,1,0:T(8,128)(2,1)S(1)}, bf16[2,72,512]{2,1,0:T(8,128)(2,1)S(1)}, u32[]{:S(2)}, u32[]{:S(2)}) collective-permute-start(bf16[2,72,512]{2,1,0:T(8,128)(2,1)S(1)} %get-tuple-element.62), channel_id=1, source_target_pairs={{1,2},{2,1},{3,4},{4,3},{5,6},{6,5},{9,10},{10,9},{11,12},{12,11},... | collective-permute-start | bytes 442376 | tf_op jit(solution)/shard_map/ppermute | solution.py:281
  34.2 2.4 %shard_map.88 = (f32[4,72,512]{2,1,0:T(8,128)S(1)}, bf16[4,72,512]{2,1,0:T(8,128)(2,1)S(1)}, bf16[4,128,512]{2,1,0:T(8,128)(2,1)S(1)}) custom-call(f32[5]{0:T(128)S(1)} %convert_element_type.3.flags.refs_0_, bf16[4,72,512]{2,1,0:T(8,128)(2,1)S(1)} %get-tuple-element.64.own_e.refs_3_, bf16[4,72,512]{2,1,0:T(8,128)(2,1)S(1)} %get-tuple-element.66.own_i, ...), custom_call_target="tpu_custom_call" | custom-call | flops 813957120 | bytes 4194304 | tf_op jit(solution)/shard_map/pallas_call | solution.py:336
  36.6 4.9 %collective-permute-done.3.refs_1_ = bf16[2,72,512]{2,1,0:T(8,128)(2,1)S(1)} collective-permute-done((bf16[2,72,512]{2,1,0:T(8,128)(2,1)S(1)}, bf16[2,72,512]{2,1,0:T(8,128)(2,1)S(1)}, u32[]{:S(2)}, u32[]{:S(2)}) %collective-permute-start.3) | collective-permute-done | bytes 147488 | tf_op jit(solution)/shard_map/ppermute | solution.py:281
  41.5 1.9 %shard_map.89 = (f32[4,72,512]{2,1,0:T(8,128)S(1)}, bf16[4,72,512]{2,1,0:T(8,128)(2,1)S(1)}, bf16[2,72,512]{2,1,0:T(8,128)(2,1)S(1)}, bf16[2,72,512]{2,1,0:T(8,128)(2,1)S(1)}) custom-call(f32[5]{0:T(128)S(1)} %convert_element_type.3.flags.refs_0_, bf16[2,72,512]{2,1,0:T(8,128)(2,1)S(1)} %collective-permute-done.3.refs_1_, ...), custom_call_target="tpu_custom_call" | custom-call | flops 651165696 | bytes 4194304 | tf_op jit(solution)/shard_map/pallas_call | solution.py:342
  43.5 1.9 %collective-permute-start.9 = (bf16[4,72,512]{2,1,0:T(8,128)(2,1)S(1)}, bf16[4,72,512]{2,1,0:T(8,128)(2,1)S(1)}, u32[]{:S(2)}, u32[]{:S(2)}) collective-permute-start(bf16[4,72,512]{2,1,0:T(8,128)(2,1)S(1)} %get-tuple-element.79.own_e.own), channel_id=1, source_target_pairs={{8,0},{16,8},{24,16},{32,24},{40,32},{48,40},{56,48},{64,56},{72,6... | collective-permute-start | bytes 884744 | tf_op jit(solution)/shard_map/ppermute | solution.py:286
  45.4 8.7 %collective-permute-start.7 = (bf16[2,72,512]{2,1,0:T(8,128)(2,1)S(1)}, bf16[2,72,512]{2,1,0:T(8,128)(2,1)S(1)}, u32[]{:S(2)}, u32[]{:S(2)}) collective-permute-start(bf16[2,72,512]{2,1,0:T(8,128)(2,1)S(1)} %get-tuple-element.77), channel_id=1, source_target_pairs={{1,2},{2,1},{3,4},{4,3},{5,6},{6,5},{9,10},{10,9},{11,12},{12,11},... | collective-permute-start | bytes 442376 | tf_op jit(solution)/shard_map/ppermute | solution.py:281
  54.2 2.2 %collective-permute-start.12 = (bf16[4,72,512]{2,1,0:T(8,128)(2,1)S(1)}, bf16[4,72,512]{2,1,0:T(8,128)(2,1)S(1)}, u32[]{:S(2)}, u32[]{:S(2)}) collective-permute-start(bf16[4,72,512]{2,1,0:T(8,128)(2,1)S(1)} %get-tuple-element.80.own_i), channel_id=1, source_target_pairs={{8,0},{16,8},{24,16},{32,24},{40,32},{48,40},{56,48},{64,56},{72,6... | collective-permute-start | bytes 884744 | tf_op jit(solution)/shard_map/ppermute | solution.py:286
  56.4 2.0 %shard_map.90 = (f32[4,72,512]{2,1,0:T(8,128)S(1)}, bf16[4,72,512]{2,1,0:T(8,128)(2,1)S(1)}, bf16[4,128,512]{2,1,0:T(8,128)(2,1)S(1)}, bf16[6,128,512]{2,1,0:T(8,128)(2,1)S(1)}) custom-call(bf16[4,72,512]{2,1,0:T(8,128)(2,1)S(1)} %get-tuple-element.79.own_e.own, bf16[4,72,512]{2,1,0:T(8,128)(2,1)S(1)} %get-tuple-element.80.own_i, ...), custom_call_target="tpu_custom_call" | custom-call | flops 813957120 | bytes 4194304 | tf_op jit(solution)/shard_map/pallas_call | solution.py:322
  58.5 5.7 %collective-permute-start.13 = (bf16[4,72,512]{2,1,0:T(8,128)(2,1)S(1)}, bf16[4,72,512]{2,1,0:T(8,128)(2,1)S(1)}, u32[]{:S(2)}, u32[]{:S(2)}) collective-permute-start(bf16[4,72,512]{2,1,0:T(8,128)(2,1)S(1)} %get-tuple-element.91), channel_id=1, source_target_pairs={{0,8},{8,16},{16,24},{24,32},{32,40},{40,48},{48,56},{56,64},{64,7... | collective-permute-start | bytes 884744 | tf_op jit(solution)/shard_map/ppermute | solution.py:286
  64.2 2.1 %shard_map.91 = (bf16[4,72,512]{2,1,0:T(8,128)(2,1)S(1)}, bf16[4,72,512]{2,1,0:T(8,128)(2,1)S(1)}, bf16[2,72,512]{2,1,0:T(8,128)(2,1)S(1)}, bf16[2,72,512]{2,1,0...) custom-call(f32[5]{0:T(128)S(1)} %convert_element_type.3.flags.refs_0_, ...), custom_call_target="tpu_custom_call" | custom-call | flops 651165696 | bytes 4194304 | tf_op jit(solution)/shard_map/pallas_call | solution.py:326
  66.3 2.0 %collective-permute-start.14 = (bf16[4,72,512]{2,1,0:T(8,128)(2,1)S(1)}, bf16[4,72,512]{2,1,0:T(8,128)(2,1)S(1)}, u32[]{:S(2)}, u32[]{:S(2)}) collective-permute-start(bf16[4,72,512]{2,1,0:T(8,128)(2,1)S(1)} %get-tuple-element.95), channel_id=1, source_target_pairs={{0,8},{8,16},{16,24},{24,32},{32,40},{40,48},{48,56},{56,64},{64,7... | collective-permute-start | bytes 884744 | tf_op jit(solution)/shard_map/ppermute | solution.py:286
  68.3 6.2 %collective-permute-start.10 = (bf16[2,72,512]{2,1,0:T(8,128)(2,1)S(1)}, bf16[2,72,512]{2,1,0:T(8,128)(2,1)S(1)}, u32[]{:S(2)}, u32[]{:S(2)}) collective-permute-start(bf16[2,72,512]{2,1,0:T(8,128)(2,1)S(1)} %get-tuple-element.84), channel_id=1, source_target_pairs={{1,2},{2,1},{3,4},{4,3},{5,6},{6,5},{9,10},{10,9},{11,12},{12,11},... | collective-permute-start | bytes 442376 | tf_op jit(solution)/shard_map/ppermute | solution.py:281
  75.4 3.1 %shard_map.93 = (f32[4,72,512]{2,1,0:T(8,128)S(1)}, bf16[4,72,512]{2,1,0:T(8,128)(2,1)}, bf16[4,128,512]{2,1,0:T(8,128)(2,1)S(1)}) custom-call(f32[5]{0:T(128)S(1)} %convert_element_type.3.flags.refs_0_, bf16[4,72,512]{2,1,0:T(8,128)(2,1)S(1)} %get-tuple-element.86.own_e.refs_3_, bf16[4,72,512]{2,1,0:T(8,128)(2,1)S(1)} %get-tuple-element.88.own_i, ...), custom_call_target="tpu_custom_call" | custom-call | flops 813957120 | bytes 4194304 | tf_op jit(solution)/shard_map/pallas_call | solution.py:336
  78.5 6.6 %collective-permute-done.10.refs_1_ = bf16[2,72,512]{2,1,0:T(8,128)(2,1)S(1)} collective-permute-done((bf16[2,72,512]{2,1,0:T(8,128)(2,1)S(1)}, bf16[2,72,512]{2,1,0:T(8,128)(2,1)S(1)}, u32[]{:S(2)}, u32[]{:S(2)}) %collective-permute-start.10) | collective-permute-done | bytes 147488 | tf_op jit(solution)/shard_map/ppermute | solution.py:281
  85.1 3.1 %shard_map.94 = f32[69,8,512]{2,1,0:T(8,128)} custom-call(f32[5]{0:T(128)S(1)} %convert_element_type.3.flags.refs_0_, bf16[2,72,512]{2,1,0:T(8,128)(2,1)S(1)} %collective-permute-done.10.refs_1_, bf16[2,72,512]{2,1,0:T(8,128)(2,1)S(1)} %collective-permute-done.11.refs_2_, bf16[4,72,512]{2,1,0:T(8,128)(2,1)S(1)} %get-tuple-element.86.own_e.refs_3_, ...), custom_call_target="tpu_custom_call" | custom-call | flops 651165696 | bytes 4194304 | tf_op jit(solution)/shard_map/pallas_call | solution.py:344
  (41 shorter events, 3.7 us)
Async XLA Ops:
  0.0 11.7 %copy-start = (f32[1,69,8,512]{3,2,1,0:T(8,128)S(1)}, f32[1,69,8,512]{3,2,1,0:T(8,128)}, u32[]{:S(2)}) copy-start(f32[1,69,8,512]{3,2,1,0:T(8,128)} %param.10) | copy-start | bytes 3391492
  0.1 1.3 %copy-start.2 = (f32[1,69,8,512]{3,2,1,0:T(8,128)S(1)}, f32[1,69,8,512]{3,2,1,0:T(8,128)}, u32[]{:S(2)}) copy-start(f32[1,69,8,512]{3,2,1,0:T(8,128)} %param.8) | copy-start | bytes 3391492
  1.4 10.2 %copy-start.8 = (f32[128]{0:T(128)S(1)}, f32[128]{0:T(128)}, u32[]{:S(2)}) copy-start(f32[128]{0:T(128)} %param.14) | copy-start | bytes 1540
  1.4 10.3 %copy-start.9 = (s32[1,69]{1,0:T(1,128)S(1)}, s32[1,69]{1,0:T(1,128)}, u32[]{:S(2)}) copy-start(s32[1,69]{1,0:T(1,128)} %chan_row.1) | copy-start | bytes 832
  2.3 19.1 %collective-permute-start.2 = (bf16[8,72,512]{2,1,0:T(8,128)(2,1)S(1)}, bf16[8,72,512]{2,1,0:T(8,128)(2,1)S(1)}, u32[]{:S(2)}, u32[]{:S(2)}) collective-permute-start(bf16[8,72,512]{2,1,0:T(8,128)(2,1)S(1)} %get-tuple-element.53.own_e.own_i.own), channel_id=1, source_target_pairs={{8,0},{16,8},{24,16},{32,24},{40,32},{48,40},{56,48},{64,56},{72,6... | collective-permute-start | bytes 1769480 | tf_op jit(solution)/shard_map/ppermute | solution.py:286
  4.9 16.5 %collective-permute-start = (bf16[2,72,512]{2,1,0:T(8,128)(2,1)S(1)}, bf16[2,72,512]{2,1,0:T(8,128)(2,1)S(1)}, u32[]{:S(2)}, u32[]{:S(2)}) collective-permute-start(bf16[2,72,512]{2,1,0:T(8,128)(2,1)S(1)} %get-tuple-element.51), channel_id=1, source_target_pairs={{1,2},{2,1},{3,4},{4,3},{5,6},{6,5},{9,10},{10,9},{11,12},{12,11},... | collective-permute-start | bytes 442376 | tf_op jit(solution)/shard_map/ppermute | solution.py:281
  11.6 9.8 %collective-permute-start.1 = (bf16[2,72,512]{2,1,0:T(8,128)(2,1)S(1)}, bf16[2,72,512]{2,1,0:T(8,128)(2,1)S(1)}, u32[]{:S(2)}, u32[]{:S(2)}) collective-permute-start(bf16[2,72,512]{2,1,0:T(8,128)(2,1)S(1)} %get-tuple-element.52), channel_id=1, source_target_pairs={{0,1},{1,0},{2,3},{3,2},{4,5},{5,4},{6,7},{7,6},{8,9},{9,8},{10,11... | collective-permute-start | bytes 442376 | tf_op jit(solution)/shard_map/ppermute | solution.py:282
  11.7 0.9 %copy-start.3 = (bf16[9,128,69]{1,2,0:T(8,128)(2,1)S(1)}, bf16[9,128,69]{1,2,0:T(8,128)(2,1)}, u32[]{:S(2)}) copy-start(bf16[9,128,69]{1,2,0:T(8,128)(2,1)} %param.13) | copy-start | bytes 476932
  13.9 7.5 %copy-start.7 = (s32[1,8,512]{2,1,0:T(8,128)S(1)}, s32[1,8,512]{2,1,0:T(8,128)}, u32[]{:S(2)}) copy-start(s32[1,8,512]{2,1,0:T(8,128)} %param.11) | copy-start | bytes 49156
  16.0 18.2 %collective-permute-start.5 = (bf16[4,72,512]{2,1,0:T(8,128)(2,1)S(1)}, bf16[4,72,512]{2,1,0:T(8,128)(2,1)S(1)}, u32[]{:S(2)}, u32[]{:S(2)}) collective-permute-start(bf16[4,72,512]{2,1,0:T(8,128)(2,1)S(1)} %get-tuple-element.69), channel_id=1, source_target_pairs={{0,8},{8,16},{16,24},{24,32},{32,40},{40,48},{48,56},{56,64},{64,7... | collective-permute-start | bytes 884744 | tf_op jit(solution)/shard_map/ppermute | solution.py:286
  21.4 11.6 %copy-start.1 = (f32[69,8,512]{2,1,0:T(8,128)S(1)}, f32[69,8,512]{2,1,0:T(8,128)}, u32[]{:S(2)}) copy-start(f32[69,8,512]{2,1,0:T(8,128)} %field.1) | copy-start | bytes 3391492
  21.4 11.6 %copy-start.4 = (bf16[9,128,69]{1,2,0:T(8,128)(2,1)S(1)}, bf16[9,128,69]{1,2,0:T(8,128)(2,1)}, u32[]{:S(2)}) copy-start(bf16[9,128,69]{1,2,0:T(8,128)(2,1)} %param.13) | copy-start | bytes 476932
  21.4 11.6 %copy-start.6 = (bf16[9,69,128]{2,1,0:T(8,128)(2,1)S(1)}, bf16[9,69,128]{2,1,0:T(8,128)(2,1)}, u32[]{:S(2)}) copy-start(bf16[9,69,128]{2,1,0:T(8,128)(2,1)} %w_out.3) | copy-start | bytes 476932
  23.6 18.0 %collective-permute-start.6 = (bf16[4,72,512]{2,1,0:T(8,128)(2,1)S(1)}, bf16[4,72,512]{2,1,0:T(8,128)(2,1)S(1)}, u32[]{:S(2)}, u32[]{:S(2)}) collective-permute-start(bf16[4,72,512]{2,1,0:T(8,128)(2,1)S(1)} %get-tuple-element.76), channel_id=1, source_target_pairs={{0,8},{8,16},{16,24},{24,32},{32,40},{40,48},{48,56},{56,64},{64,7... | collective-permute-start | bytes 884744 | tf_op jit(solution)/shard_map/ppermute | solution.py:286
  28.3 13.2 %collective-permute-start.3 = (bf16[2,72,512]{2,1,0:T(8,128)(2,1)S(1)}, bf16[2,72,512]{2,1,0:T(8,128)(2,1)S(1)}, u32[]{:S(2)}, u32[]{:S(2)}) collective-permute-start(bf16[2,72,512]{2,1,0:T(8,128)(2,1)S(1)} %get-tuple-element.62), channel_id=1, source_target_pairs={{1,2},{2,1},{3,4},{4,3},{5,6},{6,5},{9,10},{10,9},{11,12},{12,11},... | collective-permute-start | bytes 442376 | tf_op jit(solution)/shard_map/ppermute | solution.py:281
  32.9 8.6 %collective-permute-start.4 = (bf16[2,72,512]{2,1,0:T(8,128)(2,1)S(1)}, bf16[2,72,512]{2,1,0:T(8,128)(2,1)S(1)}, u32[]{:S(2)}, u32[]{:S(2)}) collective-permute-start(bf16[2,72,512]{2,1,0:T(8,128)(2,1)S(1)} %get-tuple-element.63), channel_id=1, source_target_pairs={{0,1},{1,0},{2,3},{3,2},{4,5},{5,4},{6,7},{7,6},{8,9},{9,8},{10,11... | collective-permute-start | bytes 442376 | tf_op jit(solution)/shard_map/ppermute | solution.py:282
  43.5 20.7 %collective-permute-start.9 = (bf16[4,72,512]{2,1,0:T(8,128)(2,1)S(1)}, bf16[4,72,512]{2,1,0:T(8,128)(2,1)S(1)}, u32[]{:S(2)}, u32[]{:S(2)}) collective-permute-start(bf16[4,72,512]{2,1,0:T(8,128)(2,1)S(1)} %get-tuple-element.79.own_e.own), channel_id=1, source_target_pairs={{8,0},{16,8},{24,16},{32,24},{40,32},{48,40},{56,48},{64,56},{72,6... | collective-permute-start | bytes 884744 | tf_op jit(solution)/shard_map/ppermute | solution.py:286
  45.4 18.8 %collective-permute-start.7 = (bf16[2,72,512]{2,1,0:T(8,128)(2,1)S(1)}, bf16[2,72,512]{2,1,0:T(8,128)(2,1)S(1)}, u32[]{:S(2)}, u32[]{:S(2)}) collective-permute-start(bf16[2,72,512]{2,1,0:T(8,128)(2,1)S(1)} %get-tuple-element.77), channel_id=1, source_target_pairs={{1,2},{2,1},{3,4},{4,3},{5,6},{6,5},{9,10},{10,9},{11,12},{12,11},... | collective-permute-start | bytes 442376 | tf_op jit(solution)/shard_map/ppermute | solution.py:281
  54.1 10.0 %collective-permute-start.8 = (bf16[2,72,512]{2,1,0:T(8,128)(2,1)S(1)}, bf16[2,72,512]{2,1,0:T(8,128)(2,1)S(1)}, u32[]{:S(2)}, u32[]{:S(2)}) collective-permute-start(bf16[2,72,512]{2,1,0:T(8,128)(2,1)S(1)} %get-tuple-element.78), channel_id=1, source_target_pairs={{0,1},{1,0},{2,3},{3,2},{4,5},{5,4},{6,7},{7,6},{8,9},{9,8},{10,11... | collective-permute-start | bytes 442376 | tf_op jit(solution)/shard_map/ppermute | solution.py:282
  54.2 20.4 %collective-permute-start.12 = (bf16[4,72,512]{2,1,0:T(8,128)(2,1)S(1)}, bf16[4,72,512]{2,1,0:T(8,128)(2,1)S(1)}, u32[]{:S(2)}, u32[]{:S(2)}) collective-permute-start(bf16[4,72,512]{2,1,0:T(8,128)(2,1)S(1)} %get-tuple-element.80.own_i), channel_id=1, source_target_pairs={{8,0},{16,8},{24,16},{32,24},{40,32},{48,40},{56,48},{64,56},{72,6... | collective-permute-start | bytes 884744 | tf_op jit(solution)/shard_map/ppermute | solution.py:286
  58.5 16.9 %collective-permute-start.13 = (bf16[4,72,512]{2,1,0:T(8,128)(2,1)S(1)}, bf16[4,72,512]{2,1,0:T(8,128)(2,1)S(1)}, u32[]{:S(2)}, u32[]{:S(2)}) collective-permute-start(bf16[4,72,512]{2,1,0:T(8,128)(2,1)S(1)} %get-tuple-element.91), channel_id=1, source_target_pairs={{0,8},{8,16},{16,24},{24,32},{32,40},{40,48},{48,56},{56,64},{64,7... | collective-permute-start | bytes 884744 | tf_op jit(solution)/shard_map/ppermute | solution.py:286
  66.3 18.8 %collective-permute-start.14 = (bf16[4,72,512]{2,1,0:T(8,128)(2,1)S(1)}, bf16[4,72,512]{2,1,0:T(8,128)(2,1)S(1)}, u32[]{:S(2)}, u32[]{:S(2)}) collective-permute-start(bf16[4,72,512]{2,1,0:T(8,128)(2,1)S(1)} %get-tuple-element.95), channel_id=1, source_target_pairs={{0,8},{8,16},{16,24},{24,32},{32,40},{40,48},{48,56},{56,64},{64,7... | collective-permute-start | bytes 884744 | tf_op jit(solution)/shard_map/ppermute | solution.py:286
  68.3 16.8 %collective-permute-start.10 = (bf16[2,72,512]{2,1,0:T(8,128)(2,1)S(1)}, bf16[2,72,512]{2,1,0:T(8,128)(2,1)S(1)}, u32[]{:S(2)}, u32[]{:S(2)}) collective-permute-start(bf16[2,72,512]{2,1,0:T(8,128)(2,1)S(1)} %get-tuple-element.84), channel_id=1, source_target_pairs={{1,2},{2,1},{3,4},{4,3},{5,6},{6,5},{9,10},{10,9},{11,12},{12,11},... | collective-permute-start | bytes 442376 | tf_op jit(solution)/shard_map/ppermute | solution.py:281
  74.5 10.6 %collective-permute-start.11 = (bf16[2,72,512]{2,1,0:T(8,128)(2,1)S(1)}, bf16[2,72,512]{2,1,0:T(8,128)(2,1)S(1)}, u32[]{:S(2)}, u32[]{:S(2)}) collective-permute-start(bf16[2,72,512]{2,1,0:T(8,128)(2,1)S(1)} %get-tuple-element.85), channel_id=1, source_target_pairs={{0,1},{1,0},{2,3},{3,2},{4,5},{5,4},{6,7},{7,6},{8,9},{9,8},{10,11... | collective-permute-start | bytes 442376 | tf_op jit(solution)/shard_map/ppermute | solution.py:282
  (1 other events, 0.9 us)
